TPU v7x, 32 devices: a whole 2x2x4 slice. The times are simulated.
32 devices in a mesh: group: 2 (over y), attn: 4 (over z), sect: 2 (over x), pair: 2 (over core).
Axes of the slice: x: 2, y: 2, z: 4, core: 2. Of those that a mesh axis runs over, the one named last changes fastest.
Arguments:
- queries: bfloat16 [512, 4096], P(('group', 'attn'), ('sect', 'pair')), parts along dimension 0, may hold values from -200 to 200
- kv_pool: bfloat16 [4, 8, 128, 256], P('sect', ('group', 'attn')), parts along dimension 1, may hold values from -8 to 8
- block_list: int32 [8, 2], P(('group', 'attn')), parts along dimension 0, may hold values from 0 to 3, as said below
- cache_len: int32 [8], P(('group', 'attn')), parts along dimension 0, may hold values from 128 to 256, as said below
- out_weight: bfloat16 [4096, 2048], P(('sect', 'pair'), 'attn'), may hold values from -0.09375 to 0.09375
- residual: bfloat16 [512, 2048], P(('group', 'attn', 'sect', 'pair')), parts along dimension 0, may hold values from -4 to 4
- norm_gain: float32 [2048], replicated, may hold values from 0.1 to 1.9
- router: bfloat16 [2048, 8], replicated, may hold values from -50 to 50
- expert_ids: int32 [512, 4], P(('group', 'attn', 'sect', 'pair')), parts along dimension 0, may hold values from 0 to 7, all different within a row; in each aligned block of 16 rows (0 to 15, 16 to 31, ...) at most 16 rows name the same one
- w_gate: bfloat16 [8, 2048, 768], P(('attn', 'pair'), None, 'sect'), may hold values from -0.125 to 0.125
- w_up: bfloat16 [8, 2048, 768], P(('attn', 'pair'), None, 'sect'), may hold values from -0.125 to 0.125
- w_down: bfloat16 [8, 768, 2048], P(('attn', 'pair'), None, 'sect'), may hold values from -0.21875 to 0.21875
Outputs:
- layer_out: bfloat16 [512, 2048], P(('group', 'attn', 'sect', 'pair')), parts along dimension 0
There are 2 independent parts, one for each index of `group`. A program takes and returns all parts, laid end to end along the dimension named above; an argument that names none is the same for every part. Nothing has to cross between parts.
Inputs may be any that keep to these rules, and one draw needn't show every extreme that they name: `block_list`: A group's 2 blocks are distinct, and every block of the pool is listed by some group. `cache_len`: some group has 256 live positions and some group 128. `expert_ids`: each row names 4 different experts; among the rows of one device no expert is named by more than 16 rows, a bound that some block reaches.
All inputs are finite; a program needn't handle non-finite values.
Results may differ from a plain program's by a relative error of at most 0.013.
Values may be sent and summed in bfloat16 or wider, within the bound.
No kernel may reach another device: no remote copies, remote signals or barrier semaphores. Data moves between devices by JAX's collectives and lax.ppermute only.
A program may use at most 64 MiB of HBM per device.

v0:
```python
import functools
import math

import jax
import jax.numpy as jnp
from jax import lax
from jax.experimental import pallas as pl
from jax.experimental.pallas import tpu as pltpu
from jax.sharding import PartitionSpec as P


HEADS = 32
KV_HEADS = 4
HEAD_DIM = 128


VMEM = pl.BlockSpec(memory_space=pltpu.VMEM)


def routed_layer(
    queries,
    kv_pool,
    block_list,
    cache_len,
    out_weight,
    residual,
    norm_gain,
    router,
    expert_ids,
    w_gate,
    w_up,
    w_down,
):
    head_dim = HEAD_DIM
    per_kv = HEADS // KV_HEADS
    group_rows, head_cols = queries.shape
    local_heads = head_cols // head_dim
    pool_all = lax.all_gather(kv_pool, "attn", axis=1, tiled=True)
    picked = jnp.take(pool_all, block_list[0], axis=1)
    kv_local = lax.axis_index("pair") * local_heads // per_kv
    chosen = lax.dynamic_index_in_dim(picked, kv_local, 0, keepdims=False)
    chosen = chosen.reshape(-1, 2 * head_dim)
    key_rows = chosen[:, :head_dim]
    values = chosen[:, head_dim:]
    query_heads = queries.reshape(group_rows, local_heads, head_dim)
    scores = jnp.einsum(
        "rhd,td->rht", query_heads, key_rows, preferred_element_type=jnp.float32
    ) / math.sqrt(head_dim)
    live_mask = jnp.arange(key_rows.shape[0]) < cache_len[0]
    scores = jnp.where(live_mask, scores, -jnp.inf)
    row_top = jnp.max(scores, axis=-1, keepdims=True)
    lifted = jnp.exp(scores - row_top)
    row_total = jnp.sum(lifted, axis=-1)
    soft_weights = lifted.astype(jnp.bfloat16)
    mixed_heads = (
        jnp.einsum("rht,td->rhd", soft_weights, values, preferred_element_type=jnp.float32)
        / row_total[..., None]
    )
    attended = mixed_heads.reshape(group_rows, head_cols).astype(jnp.bfloat16)
    partial_value = jnp.dot(
        attended,
        lax.all_gather(out_weight, "attn", axis=1, tiled=True),
        preferred_element_type=jnp.float32,
    )
    summed = lax.psum_scatter(partial_value, ("sect", "pair"), scatter_dimension=0, tiled=True)
    mixed_f32 = residual.astype(jnp.float32) + summed
    mixed_rows = mixed_f32.astype(jnp.bfloat16)
    mixed_f32 = mixed_rows.astype(jnp.float32)
    normed = (
        mixed_f32
        * lax.rsqrt(jnp.mean(mixed_f32 * mixed_f32, axis=-1, keepdims=True) + 1e-06)
        * norm_gain
    ).astype(jnp.bfloat16)
    logits = jnp.dot(normed, router, preferred_element_type=jnp.float32)
    chosen_logits = jnp.take_along_axis(logits, expert_ids, axis=1)
    route_weights = jax.nn.softmax(chosen_logits, axis=-1)
    row_count, top_count = expert_ids.shape
    expert_count = router.shape[1]
    model_width = residual.shape[1]
    capacity = max(2, row_count * top_count // expert_count * 2)
    flat_ids = expert_ids.reshape(-1)
    onehot = (flat_ids[:, None] == jnp.arange(expert_count, dtype=jnp.int32)[None, :]).astype(
        jnp.int32
    )
    earlier = jnp.cumsum(onehot, axis=0) - onehot
    slot_index = jnp.sum(earlier * onehot, axis=1)
    source = jnp.repeat(jnp.arange(row_count, dtype=jnp.int32), top_count)
    outgoing = (
        jnp.zeros((expert_count, capacity, model_width), jnp.bfloat16)
        .at[flat_ids, slot_index]
        .set(normed[source])
    )
    received = lax.all_to_all(outgoing, ("attn", "pair"), split_axis=0, concat_axis=0, tiled=True)
    sections = lax.axis_size("sect")
    every_section = lax.all_gather(received, "sect", axis=0, tiled=True)
    tokens_in = every_section.reshape(-1, model_width)
    gate_val = jnp.dot(tokens_in, w_gate[0], preferred_element_type=jnp.float32)
    up_val = jnp.dot(tokens_in, w_up[0], preferred_element_type=jnp.float32)
    part_hidden = (jax.nn.silu(gate_val) * up_val).astype(jnp.bfloat16)
    hidden = lax.all_gather(part_hidden, "sect", axis=1, tiled=True)
    out_slice = jnp.dot(hidden, w_down[0], preferred_element_type=jnp.float32).astype(jnp.bfloat16)
    out_slice = out_slice.reshape(sections, expert_count, capacity, model_width // sections)
    segmented = lax.all_to_all(out_slice, "sect", split_axis=0, concat_axis=3, tiled=True)
    returned = lax.all_to_all(
        segmented[0], ("attn", "pair"), split_axis=0, concat_axis=0, tiled=True
    )
    gathered = (
        returned[flat_ids, slot_index]
        .reshape(row_count, top_count, model_width)
        .astype(jnp.float32)
    )
    joined = jnp.sum(route_weights[:, :, None] * gathered, axis=1)
    return (mixed_f32 + joined).astype(jnp.bfloat16)


def rotate(value, axis, step):
    size = lax.axis_size(axis)
    return lax.ppermute(value, axis, [(i, (i + step) % size) for i in range(size)])


def swap(value, axis, mask):
    size = lax.axis_size(axis)
    return lax.ppermute(value, axis, [(i, i ^ mask) for i in range(size)])


def anchor_kernel(out_ref):
    out_ref[...] = jnp.zeros_like(out_ref)


def pack_kernel(attn, sect, *refs):
    _, q_ref, kv_ref, list_ref, len_ref, res_ref, ids_ref, down_ref, *refs = refs
    own_ref, far_ref, near_ref, q_out, *downs = refs
    my_attn, my_sect = lax.axis_index("attn"), lax.axis_index("sect")
    q_out[...] = q_ref[...]
    ff = downs[0].shape[0]
    for i in range(sect):
        start = pl.multiple_of(lax.rem(my_sect + i, sect) * ff, ff)
        downs[i][...] = down_ref[pl.ds(start, ff), :]
    per_dev = res_ref.shape[0]
    top = ids_ref.shape[0]
    width = res_ref.shape[1] // attn
    _, blocks, keys, kv_cols = kv_ref.shape
    folds = width // kv_cols
    local_heads = HEADS // (lax.axis_size("sect") * lax.axis_size("pair"))
    kv_local = lax.axis_index("pair") * local_heads // (HEADS // KV_HEADS)
    lane = lax.broadcasted_iota(jnp.int32, (per_dev, kv_cols - 128), 1)
    facts = jnp.zeros((per_dev, kv_cols - 128), jnp.int32)
    list_len = list_ref.shape[1]
    for j in range(list_len):
        facts = jnp.where(lane == j, list_ref[:, j : j + 1], facts)
    facts = jnp.where(lane == list_len, len_ref[...] // 128, facts)
    facts = jnp.where(lane == list_len + 1, lax.rem(len_ref[...], 128), facts)
    facts = facts.astype(jnp.float32).astype(jnp.bfloat16)
    eye = (
        lax.broadcasted_iota(jnp.int32, (per_dev, per_dev), 0)
        == lax.broadcasted_iota(jnp.int32, (per_dev, per_dev), 1)
    )
    ids = lax.dot_general(
        eye.astype(jnp.float32).astype(jnp.bfloat16),
        ids_ref[...].astype(jnp.float32).astype(jnp.bfloat16),
        (((1,), (1,)), ((), ())),
        preferred_element_type=jnp.float32,
    )
    ids = jnp.concatenate([ids, jnp.zeros((per_dev, 128 - top), jnp.float32)], axis=1)
    named = jnp.concatenate([ids.astype(jnp.bfloat16), facts], axis=1)

    def put_slice(ref, row, receiver):
        for f in range(folds):
            start = pl.multiple_of(receiver * width + f * kv_cols, kv_cols)
            ref[row + f * per_dev : row + (f + 1) * per_dev, :] = res_ref[:, pl.ds(start, kv_cols)]

    first = folds * per_dev
    after = first + blocks * keys
    for ref, mask in ((own_ref, 0), (far_ref, 2), (near_ref, 1)):
        put_slice(ref, 0, my_attn ^ mask)
        for b in range(blocks):
            ref[first + b * keys : first + (b + 1) * keys, :] = kv_ref[kv_local, b]
        ref[after : after + per_dev, :] = named
    put_slice(far_ref, after + per_dev, my_attn ^ 3)


def attend_kernel(attn, sect, pair, list_len, blocks, keys, *refs):
    q_refs, refs = refs[:attn], refs[attn:]
    pack_refs, refs = refs[:attn], refs[attn:]
    w_ref, refs = refs[0], refs[1:]
    part_refs, refs = refs[:pair], refs[pair:]
    ids_ref, pool, attended, split = refs
    per_dev = ids_ref.shape[0]
    rows, head_cols = q_refs[0].shape
    kv_cols = pack_refs[0].shape[1]
    width = w_ref.shape[1]
    heads = head_cols // HEAD_DIM
    folds = width // kv_cols
    me, my_sect, my_pair = (lax.axis_index(n) for n in ("attn", "sect", "pair"))
    lane = lax.broadcasted_iota(jnp.int32, (1, kv_cols - 128), 1)
    cache_at = [0 if k == 3 else folds * per_dev for k in range(attn)]
    named_at = [at + blocks * keys for at in cache_at]
    slice_at = [named_at[k] + per_dev if k == 3 else 0 for k in range(attn)]
    lists, lives = [], []
    for k in range(attn):
        group = me ^ k
        for b in range(blocks):
            at = cache_at[k] + b * keys
            pool[group * blocks + b] = pack_refs[k][at : at + keys, :]
        facts = pack_refs[k][named_at[k] : named_at[k] + per_dev, 128:]
        facts = facts.astype(jnp.float32)[0:1, :]

        def fact(j, facts=facts):
            return jnp.sum(jnp.where(lane == j, facts, 0.0)).astype(jnp.int32)

        lists.append([fact(j) for j in range(list_len)])
        lives.append(fact(list_len) * 128 + fact(list_len + 1))
    for k in range(attn):
        group = me ^ k
        picked = [pool[index] for index in lists[k]]
        key_rows = jnp.concatenate([p[:, :HEAD_DIM] for p in picked], axis=0)
        values = jnp.concatenate([p[:, HEAD_DIM:] for p in picked], axis=0)
        q_all = q_refs[k][...]
        stacked = jnp.concatenate(
            [q_all[:, h * HEAD_DIM : (h + 1) * HEAD_DIM] for h in range(heads)], axis=0
        )
        scores = lax.dot_general(
            stacked, key_rows, (((1,), (1,)), ((), ())), preferred_element_type=jnp.float32
        ) / math.sqrt(HEAD_DIM)
        where = lax.broadcasted_iota(jnp.int32, scores.shape, 1)
        scores = jnp.where(where < lives[k], scores, -jnp.inf)
        top = jnp.max(scores, axis=-1, keepdims=True)
        lifted = jnp.exp(scores - top)
        total = jnp.sum(lifted, axis=-1, keepdims=True)
        mixed = (
            jnp.dot(lifted.astype(jnp.bfloat16), values, preferred_element_type=jnp.float32)
            / total
        ).astype(jnp.bfloat16)
        start = pl.multiple_of(group * rows, rows)
        for h in range(heads):
            attended[pl.ds(start, rows), h * HEAD_DIM : (h + 1) * HEAD_DIM] = mixed[
                h * rows : (h + 1) * rows, :
            ]
    product = jnp.dot(attended[...], w_ref[...], preferred_element_type=jnp.float32)
    for g in range(attn):
        for s in range(sect):
            for p in range(pair):
                source = g * rows + (s * pair + p) * per_dev
                target = (s * attn + g) * per_dev
                split[p, target : target + per_dev, :] = product[source : source + per_dev, :]
    for k in range(attn):
        group = me ^ k
        target = pl.ds(pl.multiple_of((my_sect * attn + group) * per_dev, per_dev), per_dev)
        for f in range(folds):
            at = slice_at[k] + f * per_dev
            split[my_pair, target, f * kv_cols : (f + 1) * kv_cols] += pack_refs[k][
                at : at + per_dev, :
            ].astype(jnp.float32)
        lanes = pl.ds(pl.multiple_of(group * 128, 128), 128)
        ids_ref[:, lanes] = pack_refs[k][named_at[k] : named_at[k] + per_dev, :128]
    for i in range(pair):
        part_refs[i][...] = split[lax.rem(my_pair + i, pair)]


def pair_sum_kernel(pair, kept_ref, *refs):
    came, (ids_ref, total_ref, sent_ref) = refs[: pair - 1], refs[pair - 1 :]
    total = kept_ref[...]
    for ref in came:
        total = total + ref[...]
    total_ref[...] = total
    rows = total.shape[0]
    sent_ref[:rows, :] = total.astype(jnp.bfloat16)
    sent_ref[rows:, : ids_ref.shape[1]] = ids_ref[...]
    if ids_ref.shape[1] < total.shape[1]:
        sent_ref[rows:, ids_ref.shape[1] :] = jnp.zeros(
            (ids_ref.shape[0], total.shape[1] - ids_ref.shape[1]), jnp.bfloat16
        )


def sect_sum_kernel(sect, kept_ref, own_ref, *refs):
    came, (mixed_ref, sent_ref) = refs[: sect - 1], refs[sect - 1 :]
    my_sect = lax.axis_index("sect")
    total = kept_ref[...]
    rows = total.shape[0]
    per_dev = own_ref.shape[0] - rows
    for ref in came:
        total = total + ref[:rows, :].astype(jnp.float32)
    mixed = total.astype(jnp.bfloat16)
    mixed_ref[...] = mixed
    sent_ref[:rows, :] = mixed
    for i, ref in enumerate((own_ref,) + tuple(came)):
        from_sect = lax.rem(my_sect + sect - i, sect)
        place = pl.ds(pl.multiple_of(rows + from_sect * per_dev, per_dev), per_dev)
        sent_ref[place, :] = ref[rows:, :]


def expert_kernel(attn, sect, pair, per_dev, top, shift, *refs):
    piece_refs, refs = refs[: attn * pair], refs[attn * pair :]
    gain_ref, router_ref, gate_ref, up_ref, refs = *refs[:4], refs[4:]
    down_refs, refs = refs[:sect], refs[sect:]
    part_refs, refs = refs[:pair], refs[pair:]
    own_refs, (ids_all, contribution) = refs[:-2], refs[-2:]
    part = attn * per_dev
    half = part * sect
    width = piece_refs[0].shape[1]
    model = width * attn
    me, my_sect, my_pair = (lax.axis_index(n) for n in ("attn", "sect", "pair"))
    my_expert = me * pair + my_pair
    section = lax.rem(my_sect + shift, sect)
    block_rows = pl.ds(pl.multiple_of(section * part, part), part)
    rows = part * pair
    values = []
    squares = jnp.zeros((rows, 1), jnp.float32)
    for k in range(attn):
        value = jnp.concatenate(
            [piece_refs[j * attn + k][block_rows, :] for j in range(pair)], axis=0
        ).astype(jnp.float32)
        values.append(value)
        squares = squares + jnp.sum(value * value, axis=-1, keepdims=True)
    scale = lax.rsqrt(squares / model + 1e-06)
    gate = up = logits = None
    own_start = pl.multiple_of((my_sect * attn + me) * per_dev, per_dev)
    for k in range(attn):
        group = me ^ k
        cols = pl.ds(pl.multiple_of(group * width, width), width)
        lines = width // 128
        gain = jnp.concatenate(
            [gain_ref[pl.ds(group * lines + j, 1), :] for j in range(lines)], axis=1
        )
        normed = (values[k] * scale * gain).astype(jnp.bfloat16)
        parts = [
            jnp.dot(normed, ref[cols, :], preferred_element_type=jnp.float32)
            for ref in (gate_ref, up_ref)
        ] + [
            lax.dot_general(
                normed,
                router_ref[:, cols],
                (((1,), (1,)), ((), ())),
                preferred_element_type=jnp.float32,
            )
        ]
        if k == 0:
            gate, up, logits = parts
        else:
            gate, up, logits = gate + parts[0], up + parts[1], logits + parts[2]
        for own_ref in own_refs:
            own_ref[:, cols] = piece_refs[k][pl.ds(own_start, per_dev), :]
    for j in range(pair):
        names = pl.ds(pl.multiple_of(half + section * per_dev, per_dev), per_dev)
        block = piece_refs[j * attn][names, :].astype(jnp.float32)
        for g in range(attn):
            target = j * part + g * per_dev
            ids_all[target : target + per_dev, :] = block[:, g * 128 : g * 128 + top]
    ids = ids_all[...]
    lane = lax.broadcasted_iota(jnp.int32, logits.shape, 1)
    lane_f = lane.astype(jnp.float32)
    named = lane < 0
    for c in range(top):
        named = named | (ids[:, c : c + 1] == lane_f)
    chosen = jnp.where(named, logits, -jnp.inf)
    lifted = jnp.exp(chosen - jnp.max(chosen, axis=-1, keepdims=True))
    weights = lifted / jnp.sum(lifted, axis=-1, keepdims=True)
    weight = jnp.sum(jnp.where(lane == my_expert, weights, 0.0), axis=-1, keepdims=True)
    hidden = (gate / (1.0 + jnp.exp(-gate)) * up).astype(jnp.bfloat16)
    columns = down_refs[0].shape[1]
    for i in range(sect):
        from_sect = lax.rem(my_sect + sect - i, sect)
        cols = pl.ds(pl.multiple_of(from_sect * columns, columns), columns)
        contribution[:, cols] = (
            jnp.dot(hidden, down_refs[i][...], preferred_element_type=jnp.float32) * weight
        )
    part_refs[0][...] = contribution[:part, :]
    for j in range(1, pair):
        part_refs[j][...] = contribution[j * part : (j + 1) * part, :].astype(jnp.bfloat16)


def sum_kernel(kept_ref, *refs):
    *came, out_ref = refs
    total = kept_ref[...]
    for ref in came:
        total = total + ref[...].astype(jnp.float32)
    out_ref[...] = total.astype(out_ref.dtype)


def split_kernel(attn, kept_ref, *refs):
    came, outs = refs[:-attn], refs[-attn:]
    me = lax.axis_index("attn")
    part = kept_ref.shape[0] // attn
    for i in range(attn):
        rows = pl.ds(pl.multiple_of((me ^ i) * part, part), part)
        total = kept_ref[rows, :]
        for ref in came:
            total = total + ref[rows, :].astype(jnp.float32)
        outs[i][...] = total.astype(outs[i].dtype)


def call(kernel, operands, outs, scratch=(), limit=4 << 20, flops=1 << 20):
    moved = sum(x.size * x.dtype.itemsize for x in operands)
    return pl.pallas_call(
        kernel,
        out_shape=outs,
        in_specs=[VMEM] * len(operands),
        out_specs=jax.tree.map(lambda _: VMEM, outs),
        scratch_shapes=list(scratch),
        compiler_params=pltpu.CompilerParams(vmem_limit_bytes=limit),
        cost_estimate=pl.CostEstimate(flops=flops, bytes_accessed=moved, transcendentals=0),
    )(*operands)


def dense_layer(
    queries,
    kv_pool,
    block_list,
    cache_len,
    out_weight,
    residual,
    norm_gain,
    router,
    expert_ids,
    w_gate,
    w_up,
    w_down,
):
    attn, sect, pair = (lax.axis_size(n) for n in ("attn", "sect", "pair"))
    bf16, f32 = jnp.bfloat16, jnp.float32
    shape = jax.ShapeDtypeStruct
    rows, head_cols = queries.shape
    per_dev, model = residual.shape
    top = expert_ids.shape[1]
    width = out_weight.shape[1]
    ff = w_gate.shape[2]
    list_len = block_list.shape[1]
    _, blocks, keys, kv_cols = kv_pool.shape
    half = attn * sect * per_dev
    slice_rows = per_dev * width // kv_cols
    packed = slice_rows + blocks * keys + per_dev

    anchor = call(anchor_kernel, [], shape((8, 128), f32), flops=1 << 34)
    own_pack, far_pack, near_pack, own_q, *downs = call(
        functools.partial(pack_kernel, attn, sect),
        [
            anchor,
            queries,
            kv_pool,
            block_list,
            cache_len.reshape(1, 1),
            residual,
            expert_ids.T,
            w_down[0],
        ],
        [
            shape((packed, kv_cols), bf16),
            shape((packed + slice_rows, kv_cols), bf16),
            shape((packed, kv_cols), bf16),
            shape(queries.shape, bf16),
        ]
        + [shape((ff, w_down.shape[2]), bf16)] * sect,
    )
    far_pack = swap(far_pack, "attn", 2)
    far_q = swap(own_q, "attn", 2)
    downs = [downs[0]] + [rotate(downs[i], "sect", i) for i in range(1, sect)]
    near_pack = swap(near_pack, "attn", 1)
    near_q = swap(own_q, "attn", 1)
    last_pack = swap(far_pack[slice_rows:], "attn", 1)
    last_q = swap(far_q, "attn", 1)
    q = [own_q, near_q, far_q, last_q]
    packs = [own_pack, near_pack, far_pack, last_pack]

    parts = call(
        functools.partial(
            attend_kernel, attn, sect, pair, list_len, blocks, keys
        ),
        q + packs + [out_weight],
        [shape((half, width), f32)] * pair + [shape((per_dev, attn * 128), bf16)],
        [
            pltpu.VMEM((attn * blocks, keys, kv_cols), bf16),
            pltpu.VMEM((attn * rows, head_cols), bf16),
            pltpu.VMEM((pair, half, width), f32),
        ],
        limit=16 << 20,
    )
    total, sent = call(
        functools.partial(pair_sum_kernel, pair),
        [parts[0]] + [rotate(parts[j], "pair", j) for j in range(1, pair)] + [parts[pair]],
        [shape((half, width), f32), shape((half + per_dev, width), bf16)],
    )
    mixed, named = call(
        functools.partial(sect_sum_kernel, sect),
        [total, sent] + [rotate(sent, "sect", i) for i in range(1, sect)],
        [shape((half, width), bf16), shape((half + sect * per_dev, width), bf16)],
    )
    piece = {0: named}
    for k in range(1, attn):
        piece[k] = swap(mixed, "attn", k)
    pieces = [piece[k] for k in range(attn)]
    for j in range(1, pair):
        pieces += [rotate(piece[k], "pair", j) for k in range(attn)]

    operands = pieces + [norm_gain.reshape(-1, 128), router.T, w_gate[0], w_up[0]] + downs
    part = attn * per_dev

    def experts(shift):
        outs = call(
            functools.partial(expert_kernel, attn, sect, pair, per_dev, top, shift),
            operands,
            [shape((part, model), f32)]
            + [shape((part, model), bf16)] * (pair - 1)
            + [shape((per_dev, model), bf16)] * (shift == 0),
            [pltpu.VMEM((part * pair, top), f32), pltpu.VMEM((part * pair, model), f32)],
            limit=16 << 20,
            flops=1 << 31,
        )
        came = [rotate(outs[j], "pair", pair - j) for j in range(1, pair)]
        return outs, came

    from_sect = []
    for i in range(1, sect):
        outs, came = experts(i)
        sent = call(sum_kernel, [outs[0]] + came, shape((part, model), bf16))
        from_sect.append(rotate(sent, "sect", i))
    outs, came = experts(0)
    own_mixed = outs[pair]
    outs = call(
        functools.partial(split_kernel, attn),
        [outs[0]] + came + from_sect,
        [shape((per_dev, model), f32)] + [shape((per_dev, model), bf16)] * (attn - 1),
    )
    total = own_mixed.astype(f32) + outs[0]
    for k in range(1, attn):
        total = total + swap(outs[k], "attn", k).astype(f32)
    return total.astype(bf16)


def on_device(*operands):
    queries, expert_ids, router = operands[0], operands[8], operands[7]
    row_count, top_count = expert_ids.shape
    capacity = max(2, row_count * top_count // router.shape[1] * 2)
    local_heads = queries.shape[1] // HEAD_DIM
    one_each = operands[9].shape[0] == 1 and lax.axis_size("attn") == 4
    if capacity >= row_count and one_each and local_heads <= HEADS // KV_HEADS:
        return dense_layer(*operands)
    return routed_layer(*operands)


def solution(mesh):
    placed = (
        P(("group", "attn"), ("sect", "pair")),
        P("sect", ("group", "attn"), None, None),
        P(("group", "attn"), None),
        P(("group", "attn")),
        P(("sect", "pair"), "attn"),
        P(("group", "attn", "sect", "pair"), None),
        P(),
        P(),
        P(("group", "attn", "sect", "pair"), None),
        P(("attn", "pair"), None, "sect"),
        P(("attn", "pair"), None, "sect"),
        P(("attn", "pair"), None, "sect"),
    )
    return jax.shard_map(
        on_device,
        mesh=mesh,
        in_specs=placed,
        out_specs=P(("group", "attn", "sect", "pair"), None),
        check_vma=False,
    )
```

profile of v0, /device:TPU:0, one launch (start us, length us, event | category | flops | bytes accessed | tf_op | source)
XLA Modules:
  0.0 75.3 jit_solution(17514593362979458961)
XLA Ops:
  1.6 4.1 %collective-permute-start.1 = (bf16[64,1024]{1,0:T(8,128)(2,1)S(1)}, bf16[64,1024]{1,0:T(8,128)(2,1)S(1)}, u32[]{:S(2)}, u32[]{:S(2)}) collective-permute-start(bf16[64,1024]{1,0:T(8,128)(2,1)S(1)} %get-tuple-element.27.refs_0_), channel_id=1, source_target_pairs={{0,8},{4,12},{8,0},{12,4},{1,9},{5,13},{9,1},{13,5},{2,10},{6,14},... | collective-permute-start | bytes 393224 | tf_op jit(solution)/shard_map/ppermute | solution.py:123
  5.8 1.8 %collective-permute-start = (bf16[64,1024]{1,0:T(8,128)(2,1)S(1)}, bf16[64,1024]{1,0:T(8,128)(2,1)S(1)}, u32[]{:S(2)}, u32[]{:S(2)}) collective-permute-start(bf16[64,1024]{1,0:T(8,128)(2,1)S(1)} %get-tuple-element.27.refs_0_), channel_id=1, source_target_pairs={{0,4},{4,0},{8,12},{12,8},{1,5},{5,1},{9,13},{13,9},{2,6},{6,2},{1... | collective-permute-start | bytes 393224 | tf_op jit(solution)/shard_map/ppermute | solution.py:123
  7.7 7.5 %collective-permute-done.1.refs_2_ = bf16[64,1024]{1,0:T(8,128)(2,1)S(1)} collective-permute-done((bf16[64,1024]{1,0:T(8,128)(2,1)S(1)}, bf16[64,1024]{1,0:T(8,128)(2,1)S(1)}, u32[]{:S(2)}, u32[]{:S(2)}) %collective-permute-start.1) | collective-permute-done | bytes 131104 | tf_op jit(solution)/shard_map/ppermute | solution.py:123
  15.2 1.8 %collective-permute-start.15 = (bf16[384,1024]{1,0:T(8,128)(2,1)S(1)}, bf16[384,1024]{1,0:T(8,128)(2,1)S(1)}, u32[]{:S(2)}, u32[]{:S(2)}) collective-permute-start(bf16[384,1024]{1,0:T(8,128)(2,1)S(1)} %get-tuple-element.39), channel_id=1, source_target_pairs={{0,2},{2,0},{1,3},{3,1},{4,6},{6,4},{5,7},{7,5},{8,10},{10,8},{9,1... | collective-permute-start | bytes 2359304 | tf_op jit(solution)/shard_map/ppermute | solution.py:118
  17.0 2.0 %collective-permute-start.3 = (bf16[176,256]{1,0:T(8,128)(2,1)S(1)}, bf16[176,256]{1,0:T(8,128)(2,1)S(1)}, u32[]{:S(2)}, u32[]{:S(2)}) collective-permute-start(bf16[176,256]{1,0:T(8,128)(2,1)S(1)} %get-tuple-element.29), channel_id=1, source_target_pairs={{0,4},{4,0},{8,12},{12,8},{1,5},{5,1},{9,13},{13,9},{2,6},{6,2},{1... | collective-permute-start | bytes 270344 | tf_op jit(solution)/shard_map/ppermute | solution.py:123
  19.1 3.8 %collective-permute-done.3.refs_5_ = bf16[176,256]{1,0:T(8,128)(2,1)S(1)} collective-permute-done((bf16[176,256]{1,0:T(8,128)(2,1)S(1)}, bf16[176,256]{1,0:T(8,128)(2,1)S(1)}, u32[]{:S(2)}, u32[]{:S(2)}) %collective-permute-start.3) | collective-permute-done | bytes 90144 | tf_op jit(solution)/shard_map/ppermute | solution.py:123
  22.9 1.0 %collective-permute-done.5.refs_7_ = bf16[176,256]{1,0:T(8,128)(2,1)S(1)} collective-permute-done((bf16[176,256]{1,0:T(8,128)(2,1)S(1)}, bf16[176,256]{1,0:T(8,128)(2,1)S(1)}, u32[]{:S(2)}, u32[]{:S(2)}) %collective-permute-start.5) | collective-permute-done | bytes 90144 | tf_op jit(solution)/shard_map/ppermute | solution.py:123
  23.9 1.6 %shard_map.120 = (f32[128,512]{1,0:T(8,128)S(1)}, f32[128,512]{1,0:T(8,128)S(1)}, bf16[16,512]{1,0:T(8,128)(2,1)S(1)}) custom-call(bf16[64,1024]{1,0:T(8,128)(2,1)S(1)} %get-tuple-element.27.refs_0_, bf16[64,1024]{1,0:T(8,128)(2,1)S(1)} %collective-permute-done.refs_1_, bf16[64,1024]{1,0:T(8,128)(2,1)S(1)} %collective-permute-done.1.refs_2_, ...), custom_call_target="tpu_custom_call" | custom-call | flops 1048576 | bytes 1949696 | tf_op jit(solution)/shard_map/pallas_call | solution.py:394
  25.5 1.5 %collective-permute-done.6.refs_0_ = f32[128,512]{1,0:T(8,128)S(1)} collective-permute-done((f32[128,512]{1,0:T(8,128)S(1)}, f32[128,512]{1,0:T(8,128)S(1)}, u32[]{:S(2)}, u32[]{:S(2)}) %collective-permute-start.6) | collective-permute-done | bytes 262176 | tf_op jit(solution)/shard_map/ppermute | solution.py:118
  27.1 1.0 %collective-permute-start.7 = (bf16[144,512]{1,0:T(8,128)(2,1)S(1)}, bf16[144,512]{1,0:T(8,128)(2,1)S(1)}, u32[]{:S(2)}, u32[]{:S(2)}) collective-permute-start(bf16[144,512]{1,0:T(8,128)(2,1)S(1)} %get-tuple-element.35.own_ref), channel_id=1, source_target_pairs={{0,2},{2,0},{1,3},{3,1},{4,6},{6,4},{5,7},{7,5},{8,10},{10,8},{9,1... | collective-permute-start | bytes 442376 | tf_op jit(solution)/shard_map/ppermute | solution.py:118
  28.1 9.3 %collective-permute-done.7.refs_0_ = bf16[144,512]{1,0:T(8,128)(2,1)S(1)} collective-permute-done((bf16[144,512]{1,0:T(8,128)(2,1)S(1)}, bf16[144,512]{1,0:T(8,128)(2,1)S(1)}, u32[]{:S(2)}, u32[]{:S(2)}) %collective-permute-start.7) | collective-permute-done | bytes 147488 | tf_op jit(solution)/shard_map/ppermute | solution.py:118
  38.0 3.1 %collective-permute-start.9 = (bf16[128,512]{1,0:T(8,128)(2,1)S(1)}, bf16[128,512]{1,0:T(8,128)(2,1)S(1)}, u32[]{:S(2)}, u32[]{:S(2)}) collective-permute-start(bf16[128,512]{1,0:T(8,128)(2,1)S(1)} %get-tuple-element.37), channel_id=1, source_target_pairs={{0,8},{4,12},{8,0},{12,4},{1,9},{5,13},{9,1},{13,5},{2,10},{6,14},... | collective-permute-start | bytes 393224 | tf_op jit(solution)/shard_map/ppermute | solution.py:123
  41.2 1.2 %collective-permute-start.10 = (bf16[128,512]{1,0:T(8,128)(2,1)S(1)}, bf16[128,512]{1,0:T(8,128)(2,1)S(1)}, u32[]{:S(2)}, u32[]{:S(2)}) collective-permute-start(bf16[128,512]{1,0:T(8,128)(2,1)S(1)} %get-tuple-element.37), channel_id=1, source_target_pairs={{0,12},{4,8},{8,4},{12,0},{1,13},{5,9},{9,5},{13,1},{2,14},{6,10},... | collective-permute-start | bytes 393224 | tf_op jit(solution)/shard_map/ppermute | solution.py:123
  42.3 1.7 %collective-permute-done.8.refs_1_ = bf16[128,512]{1,0:T(8,128)(2,1)S(1)} collective-permute-done((bf16[128,512]{1,0:T(8,128)(2,1)S(1)}, bf16[128,512]{1,0:T(8,128)(2,1)S(1)}, u32[]{:S(2)}, u32[]{:S(2)}) %collective-permute-start.8) | collective-permute-done | bytes 131104 | tf_op jit(solution)/shard_map/ppermute | solution.py:123
  44.1 6.6 %collective-permute-done.9.refs_2_ = bf16[128,512]{1,0:T(8,128)(2,1)S(1)} collective-permute-done((bf16[128,512]{1,0:T(8,128)(2,1)S(1)}, bf16[128,512]{1,0:T(8,128)(2,1)S(1)}, u32[]{:S(2)}, u32[]{:S(2)}) %collective-permute-start.9) | collective-permute-done | bytes 131104 | tf_op jit(solution)/shard_map/ppermute | solution.py:123
  51.2 0.8 %collective-permute-done.13.refs_6_ = bf16[128,512]{1,0:T(8,128)(2,1)S(1)} collective-permute-done((bf16[128,512]{1,0:T(8,128)(2,1)S(1)}, bf16[128,512]{1,0:T(8,128)(2,1)S(1)}, u32[]{:S(2)}, u32[]{:S(2)}) %collective-permute-start.13) | collective-permute-done | bytes 131104 | tf_op jit(solution)/shard_map/ppermute | solution.py:118
  52.2 1.5 %shard_map.124 = (f32[64,2048]{1,0:T(8,128)S(1)}, bf16[64,2048]{1,0:T(8,128)(2,1)S(1)}) custom-call(bf16[160,512]{1,0:T(8,128)(2,1)S(1)} %get-tuple-element.36.refs_0_, bf16[128,512]{1,0:T(8,128)(2,1)S(1)} %collective-permute-done.8.refs_1_, bf16[128,512]{1,0:T(8,128)(2,1)S(1)} %collective-permute-done.9.refs_2_, ...), custom_call_target="tpu_custom_call" | custom-call | flops 2147483648 | bytes 5873664 | tf_op jit(solution)/shard_map/pallas_call | solution.py:394
  54.1 1.5 %shard_map.123 = (f32[64,2048]{1,0:T(8,128)S(1)}, bf16[64,2048]{1,0:T(8,128)(2,1)S(1)}, bf16[16,2048]{1,0:T(8,128)(2,1)S(1)}) custom-call(bf16[160,512]{1,0:T(8,128)(2,1)S(1)} %get-tuple-element.36.refs_0_, bf16[128,512]{1,0:T(8,128)(2,1)S(1)} %collective-permute-done.8.refs_1_, bf16[128,512]{1,0:T(8,128)(2,1)S(1)} %collective-permute-done.9.refs_2_, ...), custom_call_target="tpu_custom_call" | custom-call | flops 2147483648 | bytes 5873664 | tf_op jit(solution)/shard_map/pallas_call | solution.py:394
  55.9 1.6 %collective-permute-start.18 = (bf16[64,2048]{1,0:T(8,128)(2,1)S(1)}, bf16[64,2048]{1,0:T(8,128)(2,1)S(1)}, u32[]{:S(2)}, u32[]{:S(2)}) collective-permute-start(bf16[64,2048]{1,0:T(8,128)(2,1)S(1)} %shard_map.125), channel_id=1, source_target_pairs={{0,2},{2,0},{1,3},{3,1},{4,6},{6,4},{5,7},{7,5},{8,10},{10,8},{9,1... | collective-permute-start | bytes 786440 | tf_op jit(solution)/shard_map/ppermute | solution.py:118
  57.5 7.0 %collective-permute-done.18.refs_1_ = bf16[64,2048]{1,0:T(8,128)(2,1)S(1)} collective-permute-done((bf16[64,2048]{1,0:T(8,128)(2,1)S(1)}, bf16[64,2048]{1,0:T(8,128)(2,1)S(1)}, u32[]{:S(2)}, u32[]{:S(2)}) %collective-permute-start.18) | collective-permute-done | bytes 262176 | tf_op jit(solution)/shard_map/ppermute | solution.py:118
  64.6 2.1 %collective-permute-start.19 = (bf16[16,2048]{1,0:T(8,128)(2,1)S(1)}, bf16[16,2048]{1,0:T(8,128)(2,1)S(1)}, u32[]{:S(2)}, u32[]{:S(2)}) collective-permute-start(bf16[16,2048]{1,0:T(8,128)(2,1)S(1)} %get-tuple-element.46), channel_id=1, source_target_pairs={{0,4},{4,0},{8,12},{12,8},{1,5},{5,1},{9,13},{13,9},{2,6},{6,2},{1... | collective-permute-start | bytes 196616 | tf_op jit(solution)/shard_map/ppermute | solution.py:123
  66.7 1.7 %collective-permute-start.20 = (bf16[16,2048]{1,0:T(8,128)(2,1)S(1)}, bf16[16,2048]{1,0:T(8,128)(2,1)S(1)}, u32[]{:S(2)}, u32[]{:S(2)}) collective-permute-start(bf16[16,2048]{1,0:T(8,128)(2,1)S(1)} %get-tuple-element.47), channel_id=1, source_target_pairs={{0,8},{4,12},{8,0},{12,4},{1,9},{5,13},{9,1},{13,5},{2,10},{6,14},... | collective-permute-start | bytes 196616 | tf_op jit(solution)/shard_map/ppermute | solution.py:123
  68.4 1.4 %collective-permute-start.21 = (bf16[16,2048]{1,0:T(8,128)(2,1)S(1)}, bf16[16,2048]{1,0:T(8,128)(2,1)S(1)}, u32[]{:S(2)}, u32[]{:S(2)}) collective-permute-start(bf16[16,2048]{1,0:T(8,128)(2,1)S(1)} %get-tuple-element.48), channel_id=1, source_target_pairs={{0,12},{4,8},{8,4},{12,0},{1,13},{5,9},{9,5},{13,1},{2,14},{6,10},... | collective-permute-start | bytes 196616 | tf_op jit(solution)/shard_map/ppermute | solution.py:123
  69.8 4.8 %collective-permute-done.20 = bf16[16,2048]{1,0:T(8,128)(2,1)S(1)} collective-permute-done((bf16[16,2048]{1,0:T(8,128)(2,1)S(1)}, bf16[16,2048]{1,0:T(8,128)(2,1)S(1)}, u32[]{:S(2)}, u32[]{:S(2)}) %collective-permute-start.20) | collective-permute-done | bytes 65568 | tf_op jit(solution)/shard_map/ppermute | solution.py:123
  (53 shorter events, 3.9 us)
Async XLA Ops:
  1.6 13.6 %collective-permute-start.1 = (bf16[64,1024]{1,0:T(8,128)(2,1)S(1)}, bf16[64,1024]{1,0:T(8,128)(2,1)S(1)}, u32[]{:S(2)}, u32[]{:S(2)}) collective-permute-start(bf16[64,1024]{1,0:T(8,128)(2,1)S(1)} %get-tuple-element.27.refs_0_), channel_id=1, source_target_pairs={{0,8},{4,12},{8,0},{12,4},{1,9},{5,13},{9,1},{13,5},{2,10},{6,14},... | collective-permute-start | bytes 393224 | tf_op jit(solution)/shard_map/ppermute | solution.py:123
  5.7 13.3 %collective-permute-start.4 = (bf16[208,256]{1,0:T(8,128)(2,1)S(1)}, bf16[208,256]{1,0:T(8,128)(2,1)S(1)}, u32[]{:S(2)}, u32[]{:S(2)}) collective-permute-start(bf16[208,256]{1,0:T(8,128)(2,1)S(1)} %get-tuple-element.30), channel_id=1, source_target_pairs={{0,8},{4,12},{8,0},{12,4},{1,9},{5,13},{9,1},{13,5},{2,10},{6,14},... | collective-permute-start | bytes 319496 | tf_op jit(solution)/shard_map/ppermute | solution.py:123
  5.8 17.1 %collective-permute-start = (bf16[64,1024]{1,0:T(8,128)(2,1)S(1)}, bf16[64,1024]{1,0:T(8,128)(2,1)S(1)}, u32[]{:S(2)}, u32[]{:S(2)}) collective-permute-start(bf16[64,1024]{1,0:T(8,128)(2,1)S(1)} %get-tuple-element.27.refs_0_), channel_id=1, source_target_pairs={{0,4},{4,0},{8,12},{12,8},{1,5},{5,1},{9,13},{13,9},{2,6},{6,2},{1... | collective-permute-start | bytes 393224 | tf_op jit(solution)/shard_map/ppermute | solution.py:123
  15.2 8.7 %collective-permute-start.2 = (bf16[64,1024]{1,0:T(8,128)(2,1)S(1)}, bf16[64,1024]{1,0:T(8,128)(2,1)S(1)}, u32[]{:S(2)}, u32[]{:S(2)}) collective-permute-start(bf16[64,1024]{1,0:T(8,128)(2,1)S(1)} %collective-permute-done.1.refs_2_), channel_id=1, source_target_pairs={{0,4},{4,0},{8,12},{12,8},{1,5},{5,1},{9,13},{13,9},{2,6},{6,2},{1... | collective-permute-start | bytes 393224 | tf_op jit(solution)/shard_map/ppermute | solution.py:123
  15.2 36.0 %collective-permute-start.15 = (bf16[384,1024]{1,0:T(8,128)(2,1)S(1)}, bf16[384,1024]{1,0:T(8,128)(2,1)S(1)}, u32[]{:S(2)}, u32[]{:S(2)}) collective-permute-start(bf16[384,1024]{1,0:T(8,128)(2,1)S(1)} %get-tuple-element.39), channel_id=1, source_target_pairs={{0,2},{2,0},{1,3},{3,1},{4,6},{6,4},{5,7},{7,5},{8,10},{10,8},{9,1... | collective-permute-start | bytes 2359304 | tf_op jit(solution)/shard_map/ppermute | solution.py:118
  17.0 5.9 %collective-permute-start.3 = (bf16[176,256]{1,0:T(8,128)(2,1)S(1)}, bf16[176,256]{1,0:T(8,128)(2,1)S(1)}, u32[]{:S(2)}, u32[]{:S(2)}) collective-permute-start(bf16[176,256]{1,0:T(8,128)(2,1)S(1)} %get-tuple-element.29), channel_id=1, source_target_pairs={{0,4},{4,0},{8,12},{12,8},{1,5},{5,1},{9,13},{13,9},{2,6},{6,2},{1... | collective-permute-start | bytes 270344 | tf_op jit(solution)/shard_map/ppermute | solution.py:123
  19.0 33.2 %copy-start.8 = (bf16[1,2048,384]{2,1,0:T(8,128)(2,1)S(1)}, bf16[1,2048,384]{2,1,0:T(8,128)(2,1)}, u32[]{:S(2)}) copy-start(bf16[1,2048,384]{2,1,0:T(8,128)(2,1)} %param.22) | copy-start | bytes 4718596
  19.0 33.2 %copy-start.7 = (bf16[1,2048,384]{2,1,0:T(8,128)(2,1)S(1)}, bf16[1,2048,384]{2,1,0:T(8,128)(2,1)}, u32[]{:S(2)}) copy-start(bf16[1,2048,384]{2,1,0:T(8,128)(2,1)} %param.21) | copy-start | bytes 4718596
  19.1 4.8 %collective-permute-start.5 = (bf16[176,256]{1,0:T(8,128)(2,1)S(1)}, bf16[176,256]{1,0:T(8,128)(2,1)S(1)}, u32[]{:S(2)}, u32[]{:S(2)}) collective-permute-start(bf16[176,256]{1,0:T(8,128)(2,1)S(1)} %slice.4), channel_id=1, source_target_pairs={{0,4},{4,0},{8,12},{12,8},{1,5},{5,1},{9,13},{13,9},{2,6},{6,2},{1... | collective-permute-start | bytes 270344 | tf_op jit(solution)/shard_map/ppermute | solution.py:123
  25.4 1.6 %collective-permute-start.6 = (f32[128,512]{1,0:T(8,128)S(1)}, f32[128,512]{1,0:T(8,128)S(1)}, u32[]{:S(2)}, u32[]{:S(2)}) collective-permute-start(f32[128,512]{1,0:T(8,128)S(1)} %get-tuple-element.32), channel_id=1, source_target_pairs={{0,1},{1,0},{2,3},{3,2},{4,5},{5,4},{6,7},{7,6},{8,9},{9,8},{10,11... | collective-permute-start | bytes 786440 | tf_op jit(solution)/shard_map/ppermute | solution.py:118
  27.1 10.3 %collective-permute-start.7 = (bf16[144,512]{1,0:T(8,128)(2,1)S(1)}, bf16[144,512]{1,0:T(8,128)(2,1)S(1)}, u32[]{:S(2)}, u32[]{:S(2)}) collective-permute-start(bf16[144,512]{1,0:T(8,128)(2,1)S(1)} %get-tuple-element.35.own_ref), channel_id=1, source_target_pairs={{0,2},{2,0},{1,3},{3,1},{4,6},{6,4},{5,7},{7,5},{8,10},{10,8},{9,1... | collective-permute-start | bytes 442376 | tf_op jit(solution)/shard_map/ppermute | solution.py:118
  37.4 6.6 %collective-permute-start.8 = (bf16[128,512]{1,0:T(8,128)(2,1)S(1)}, bf16[128,512]{1,0:T(8,128)(2,1)S(1)}, u32[]{:S(2)}, u32[]{:S(2)}) collective-permute-start(bf16[128,512]{1,0:T(8,128)(2,1)S(1)} %get-tuple-element.37), channel_id=1, source_target_pairs={{0,4},{4,0},{8,12},{12,8},{1,5},{5,1},{9,13},{13,9},{2,6},{6,2},{1... | collective-permute-start | bytes 393224 | tf_op jit(solution)/shard_map/ppermute | solution.py:123
  38.0 12.7 %collective-permute-start.9 = (bf16[128,512]{1,0:T(8,128)(2,1)S(1)}, bf16[128,512]{1,0:T(8,128)(2,1)S(1)}, u32[]{:S(2)}, u32[]{:S(2)}) collective-permute-start(bf16[128,512]{1,0:T(8,128)(2,1)S(1)} %get-tuple-element.37), channel_id=1, source_target_pairs={{0,8},{4,12},{8,0},{12,4},{1,9},{5,13},{9,1},{13,5},{2,10},{6,14},... | collective-permute-start | bytes 393224 | tf_op jit(solution)/shard_map/ppermute | solution.py:123
  41.2 9.5 %collective-permute-start.10 = (bf16[128,512]{1,0:T(8,128)(2,1)S(1)}, bf16[128,512]{1,0:T(8,128)(2,1)S(1)}, u32[]{:S(2)}, u32[]{:S(2)}) collective-permute-start(bf16[128,512]{1,0:T(8,128)(2,1)S(1)} %get-tuple-element.37), channel_id=1, source_target_pairs={{0,12},{4,8},{8,4},{12,0},{1,13},{5,9},{9,5},{13,1},{2,14},{6,10},... | collective-permute-start | bytes 393224 | tf_op jit(solution)/shard_map/ppermute | solution.py:123
  42.3 8.9 %collective-permute-start.11 = (bf16[160,512]{1,0:T(8,128)(2,1)S(1)}, bf16[160,512]{1,0:T(8,128)(2,1)S(1)}, u32[]{:S(2)}, u32[]{:S(2)}) collective-permute-start(bf16[160,512]{1,0:T(8,128)(2,1)S(1)} %get-tuple-element.36.refs_0_), channel_id=1, source_target_pairs={{0,1},{1,0},{2,3},{3,2},{4,5},{5,4},{6,7},{7,6},{8,9},{9,8},{10,11... | collective-permute-start | bytes 491528 | tf_op jit(solution)/shard_map/ppermute | solution.py:118
  44.1 7.1 %collective-permute-start.12 = (bf16[128,512]{1,0:T(8,128)(2,1)S(1)}, bf16[128,512]{1,0:T(8,128)(2,1)S(1)}, u32[]{:S(2)}, u32[]{:S(2)}) collective-permute-start(bf16[128,512]{1,0:T(8,128)(2,1)S(1)} %collective-permute-done.8.refs_1_), channel_id=1, source_target_pairs={{0,1},{1,0},{2,3},{3,2},{4,5},{5,4},{6,7},{7,6},{8,9},{9,8},{10,11... | collective-permute-start | bytes 393224 | tf_op jit(solution)/shard_map/ppermute | solution.py:118
  50.7 1.3 %collective-permute-start.13 = (bf16[128,512]{1,0:T(8,128)(2,1)S(1)}, bf16[128,512]{1,0:T(8,128)(2,1)S(1)}, u32[]{:S(2)}, u32[]{:S(2)}) collective-permute-start(bf16[128,512]{1,0:T(8,128)(2,1)S(1)} %collective-permute-done.9.refs_2_), channel_id=1, source_target_pairs={{0,1},{1,0},{2,3},{3,2},{4,5},{5,4},{6,7},{7,6},{8,9},{9,8},{10,11... | collective-permute-start | bytes 393224 | tf_op jit(solution)/shard_map/ppermute | solution.py:118
  50.7 1.5 %collective-permute-start.14 = (bf16[128,512]{1,0:T(8,128)(2,1)S(1)}, bf16[128,512]{1,0:T(8,128)(2,1)S(1)}, u32[]{:S(2)}, u32[]{:S(2)}) collective-permute-start(bf16[128,512]{1,0:T(8,128)(2,1)S(1)} %collective-permute-done.10.refs_3_), channel_id=1, source_target_pairs={{0,1},{1,0},{2,3},{3,2},{4,5},{5,4},{6,7},{7,6},{8,9},{9,8},{10,11... | collective-permute-start | bytes 393224 | tf_op jit(solution)/shard_map/ppermute | solution.py:118
  53.7 2.1 %collective-permute-start.17 = (bf16[64,2048]{1,0:T(8,128)(2,1)S(1)}, bf16[64,2048]{1,0:T(8,128)(2,1)S(1)}, u32[]{:S(2)}, u32[]{:S(2)}) collective-permute-start(bf16[64,2048]{1,0:T(8,128)(2,1)S(1)} %get-tuple-element.44), channel_id=1, source_target_pairs={{0,1},{1,0},{2,3},{3,2},{4,5},{5,4},{6,7},{7,6},{8,9},{9,8},{10,11... | collective-permute-start | bytes 786440 | tf_op jit(solution)/shard_map/ppermute | solution.py:118
  55.6 1.9 %collective-permute-start.16 = (bf16[64,2048]{1,0:T(8,128)(2,1)S(1)}, bf16[64,2048]{1,0:T(8,128)(2,1)S(1)}, u32[]{:S(2)}, u32[]{:S(2)}) collective-permute-start(bf16[64,2048]{1,0:T(8,128)(2,1)S(1)} %get-tuple-element.42), channel_id=1, source_target_pairs={{0,1},{1,0},{2,3},{3,2},{4,5},{5,4},{6,7},{7,6},{8,9},{9,8},{10,11... | collective-permute-start | bytes 786440 | tf_op jit(solution)/shard_map/ppermute | solution.py:118
  55.9 8.6 %collective-permute-start.18 = (bf16[64,2048]{1,0:T(8,128)(2,1)S(1)}, bf16[64,2048]{1,0:T(8,128)(2,1)S(1)}, u32[]{:S(2)}, u32[]{:S(2)}) collective-permute-start(bf16[64,2048]{1,0:T(8,128)(2,1)S(1)} %shard_map.125), channel_id=1, source_target_pairs={{0,2},{2,0},{1,3},{3,1},{4,6},{6,4},{5,7},{7,5},{8,10},{10,8},{9,1... | collective-permute-start | bytes 786440 | tf_op jit(solution)/shard_map/ppermute | solution.py:118
  64.6 5.2 %collective-permute-start.19 = (bf16[16,2048]{1,0:T(8,128)(2,1)S(1)}, bf16[16,2048]{1,0:T(8,128)(2,1)S(1)}, u32[]{:S(2)}, u32[]{:S(2)}) collective-permute-start(bf16[16,2048]{1,0:T(8,128)(2,1)S(1)} %get-tuple-element.46), channel_id=1, source_target_pairs={{0,4},{4,0},{8,12},{12,8},{1,5},{5,1},{9,13},{13,9},{2,6},{6,2},{1... | collective-permute-start | bytes 196616 | tf_op jit(solution)/shard_map/ppermute | solution.py:123
  66.7 7.9 %collective-permute-start.20 = (bf16[16,2048]{1,0:T(8,128)(2,1)S(1)}, bf16[16,2048]{1,0:T(8,128)(2,1)S(1)}, u32[]{:S(2)}, u32[]{:S(2)}) collective-permute-start(bf16[16,2048]{1,0:T(8,128)(2,1)S(1)} %get-tuple-element.47), channel_id=1, source_target_pairs={{0,8},{4,12},{8,0},{12,4},{1,9},{5,13},{9,1},{13,5},{2,10},{6,14},... | collective-permute-start | bytes 196616 | tf_op jit(solution)/shard_map/ppermute | solution.py:123
  68.4 6.2 %collective-permute-start.21 = (bf16[16,2048]{1,0:T(8,128)(2,1)S(1)}, bf16[16,2048]{1,0:T(8,128)(2,1)S(1)}, u32[]{:S(2)}, u32[]{:S(2)}) collective-permute-start(bf16[16,2048]{1,0:T(8,128)(2,1)S(1)} %get-tuple-element.48), channel_id=1, source_target_pairs={{0,12},{4,8},{8,4},{12,0},{1,13},{5,9},{9,5},{13,1},{2,14},{6,10},... | collective-permute-start | bytes 196616 | tf_op jit(solution)/shard_map/ppermute | solution.py:123
  (9 other events, 98.2 us)
where the time goes:
time: 75.4 us; the launch traced here: 75.3 us
  waiting for transfers between devices  44.3 us (59%)
  starting transfers between devices  23.8 us (32%)
  Pallas kernels  4.9 us (6%)
  between operations  0.96 us (1%)
    ppermute x12, waiting for transfers between devices, swap(): return lax.ppermute(value, axis, [(i, i ^ mask) for i in range(size)])  25.4 us
    ppermute x10, waiting for transfers between devices, rotate(): lax.ppermute(value, axis, [(i, (i + step) % size) for i in range(size)])  18.9 us
    ppermute x12, starting transfers between devices, swap(): return lax.ppermute(value, axis, [(i, i ^ mask) for i in range(size)])  18.2 us
    ppermute x10, starting transfers between devices, rotate(): lax.ppermute(value, axis, [(i, (i + step) % size) for i in range(size)])  5.63 us
    pallas_call x9, Pallas kernels, call(): pl.pallas_call(kernel, out_shape=outs, in_specs=[VMEM] * len(operands), o...  4.9 us
  transfers between devices with their start and end apart: 22, of which 11 were waited for; matrix products, arithmetic and copies ran while one was open for 0% of the time, Pallas kernels for 4%

commit v1 on v0

--- a/solution.py
+++ b/solution.py
@@ -257,64 +257,61 @@
         part_refs[i][...] = split[lax.rem(my_pair + i, pair)]
 
 
-def pair_sum_kernel(pair, kept_ref, *refs):
-    came, (ids_ref, total_ref, sent_ref) = refs[: pair - 1], refs[pair - 1 :]
+def pair_sum_kernel(sect, pair, kept_ref, *refs):
+    came, ids_ref, refs = refs[: pair - 1], refs[pair - 1], refs[pair:]
+    totals, sents = refs[:sect], refs[sect:]
+    my_sect = lax.axis_index("sect")
+    part = kept_ref.shape[0] // sect
+    for i in range(sect):
+        rows = pl.ds(pl.multiple_of(lax.rem(my_sect + i, sect) * part, part), part)
+        total = kept_ref[rows, :]
+        for ref in came:
+            total = total + ref[rows, :]
+        totals[i][...] = total
+        sents[i][:part, :] = total.astype(jnp.bfloat16)
+    named = ids_ref.shape[1]
+    sents[0][part:, :named] = ids_ref[...]
+    if named < kept_ref.shape[1]:
+        sents[0][part:, named:] = jnp.zeros(
+            (ids_ref.shape[0], kept_ref.shape[1] - named), jnp.bfloat16
+        )
+
+
+def sect_sum_kernel(kept_ref, names_ref, *refs):
+    *came, mixed_ref, sent_ref = refs
+    part = kept_ref.shape[0]
     total = kept_ref[...]
     for ref in came:
-        total = total + ref[...]
-    total_ref[...] = total
-    rows = total.shape[0]
-    sent_ref[:rows, :] = total.astype(jnp.bfloat16)
-    sent_ref[rows:, : ids_ref.shape[1]] = ids_ref[...]
-    if ids_ref.shape[1] < total.shape[1]:
-        sent_ref[rows:, ids_ref.shape[1] :] = jnp.zeros(
-            (ids_ref.shape[0], total.shape[1] - ids_ref.shape[1]), jnp.bfloat16
-        )
-
-
-def sect_sum_kernel(sect, kept_ref, own_ref, *refs):
-    came, (mixed_ref, sent_ref) = refs[: sect - 1], refs[sect - 1 :]
-    my_sect = lax.axis_index("sect")
-    total = kept_ref[...]
-    rows = total.shape[0]
-    per_dev = own_ref.shape[0] - rows
-    for ref in came:
-        total = total + ref[:rows, :].astype(jnp.float32)
+        total = total + ref[:part, :].astype(jnp.float32)
     mixed = total.astype(jnp.bfloat16)
     mixed_ref[...] = mixed
-    sent_ref[:rows, :] = mixed
-    for i, ref in enumerate((own_ref,) + tuple(came)):
-        from_sect = lax.rem(my_sect + sect - i, sect)
-        place = pl.ds(pl.multiple_of(rows + from_sect * per_dev, per_dev), per_dev)
-        sent_ref[place, :] = ref[rows:, :]
-
-
-def expert_kernel(attn, sect, pair, per_dev, top, shift, *refs):
+    sent_ref[:part, :] = mixed
+    sent_ref[part:, :] = names_ref[part:, :]
+
+
+def expert_kernel(attn, sect, pair, per_dev, top, *refs):
     piece_refs, refs = refs[: attn * pair], refs[attn * pair :]
     gain_ref, router_ref, gate_ref, up_ref, refs = *refs[:4], refs[4:]
     down_refs, refs = refs[:sect], refs[sect:]
     part_refs, refs = refs[:pair], refs[pair:]
     own_refs, (ids_all, contribution) = refs[:-2], refs[-2:]
     part = attn * per_dev
-    half = part * sect
     width = piece_refs[0].shape[1]
     model = width * attn
     me, my_sect, my_pair = (lax.axis_index(n) for n in ("attn", "sect", "pair"))
     my_expert = me * pair + my_pair
-    section = lax.rem(my_sect + shift, sect)
-    block_rows = pl.ds(pl.multiple_of(section * part, part), part)
     rows = part * pair
     values = []
     squares = jnp.zeros((rows, 1), jnp.float32)
     for k in range(attn):
         value = jnp.concatenate(
-            [piece_refs[j * attn + k][block_rows, :] for j in range(pair)], axis=0
+            [piece_refs[j * attn + k][:part, :] for j in range(pair)], axis=0
         ).astype(jnp.float32)
         values.append(value)
         squares = squares + jnp.sum(value * value, axis=-1, keepdims=True)
     scale = lax.rsqrt(squares / model + 1e-06)
     gate = up = logits = None
-    own_start = pl.multiple_of((my_sect * attn + me) * per_dev, per_dev)
+    own_start = pl.multiple_of(me * per_dev, per_dev)
     for k in range(attn):
         group = me ^ k
         cols = pl.ds(pl.multiple_of(group * width, width), width)
@@ -341,8 +338,7 @@
         for own_ref in own_refs:
             own_ref[:, cols] = piece_refs[k][pl.ds(own_start, per_dev), :]
     for j in range(pair):
-        names = pl.ds(pl.multiple_of(half + section * per_dev, per_dev), per_dev)
-        block = piece_refs[j * attn][names, :].astype(jnp.float32)
+        block = piece_refs[j * attn][part:, :].astype(jnp.float32)
         for g in range(attn):
             target = j * part + g * per_dev
             ids_all[target : target + per_dev, :] = block[:, g * 128 : g * 128 + top]
@@ -474,30 +470,40 @@
         ],
         limit=16 << 20,
     )
-    total, sent = call(
-        functools.partial(pair_sum_kernel, pair),
-        [parts[0]] + [rotate(parts[j], "pair", j) for j in range(1, pair)] + [parts[pair]],
-        [shape((half, width), f32), shape((half + per_dev, width), bf16)],
-    )
-    mixed, named = call(
-        functools.partial(sect_sum_kernel, sect),
-        [total, sent] + [rotate(sent, "sect", i) for i in range(1, sect)],
-        [shape((half, width), bf16), shape((half + sect * per_dev, width), bf16)],
-    )
-    piece = {0: named}
-    for k in range(1, attn):
-        piece[k] = swap(mixed, "attn", k)
-    pieces = [piece[k] for k in range(attn)]
-    for j in range(1, pair):
-        pieces += [rotate(piece[k], "pair", j) for k in range(attn)]
-
-    operands = pieces + [norm_gain.reshape(-1, 128), router.T, w_gate[0], w_up[0]] + downs
     part = attn * per_dev
+    sums = call(
+        functools.partial(pair_sum_kernel, sect, pair),
+        [parts[0]]
+        + [rotate(parts[j], "pair", j) for j in range(1, pair)]
+        + [parts[pair]],
+        [shape((part, width), f32)] * sect
+        + [shape((part + per_dev, width), bf16)]
+        + [shape((part, width), bf16)] * (sect - 1),
+    )
+    totals, sents = sums[:sect], sums[sect:]
+    theirs = [rotate(sents[0], "sect", sect - i) for i in range(1, sect)]
+    mine = [rotate(sents[i], "sect", i) for i in range(1, sect)]
+    operands = [norm_gain.reshape(-1, 128), router.T, w_gate[0], w_up[0]] + downs
 
     def experts(shift):
+        if shift == 0:
+            names, came = sents[0], mine
+        else:
+            names, came = theirs[shift - 1], [theirs[shift - 1]]
+        mixed, named = call(
+            sect_sum_kernel,
+            [totals[shift], names] + came,
+            [shape((part, width), bf16), shape((part + per_dev, width), bf16)],
+        )
+        piece = {0: named}
+        for k in range(1, attn):
+            piece[k] = swap(mixed, "attn", k)
+        pieces = [piece[k] for k in range(attn)]
+        for j in range(1, pair):
+            pieces += [rotate(piece[k], "pair", j) for k in range(attn)]
         outs = call(
-            functools.partial(expert_kernel, attn, sect, pair, per_dev, top, shift),
-            operands,
+            functools.partial(expert_kernel, attn, sect, pair, per_dev, top),
+            pieces + operands,
             [shape((part, model), f32)]
             + [shape((part, model), bf16)] * (pair - 1)
             + [shape((per_dev, model), bf16)] * (shift == 0),
@@ -508,21 +514,25 @@
         came = [rotate(outs[j], "pair", pair - j) for j in range(1, pair)]
         return outs, came
 
+    def reduced(shift):
+        outs, came = experts(shift)
+        sums = call(
+            functools.partial(split_kernel, attn),
+            [outs[0]] + came,
+            [shape((per_dev, model), f32)] + [shape((per_dev, model), bf16)] * (attn - 1),
+        )
+        home = [swap(sums[k], "attn", k) for k in range(1, attn)]
+        return outs, sums[0], home
+
     from_sect = []
     for i in range(1, sect):
-        outs, came = experts(i)
-        sent = call(sum_kernel, [outs[0]] + came, shape((part, model), bf16))
+        _, own, home = reduced(i)
+        sent = call(sum_kernel, [own] + home, shape((per_dev, model), bf16))
         from_sect.append(rotate(sent, "sect", i))
-    outs, came = experts(0)
-    own_mixed = outs[pair]
-    outs = call(
-        functools.partial(split_kernel, attn),
-        [outs[0]] + came + from_sect,
-        [shape((per_dev, model), f32)] + [shape((per_dev, model), bf16)] * (attn - 1),
-    )
-    total = own_mixed.astype(f32) + outs[0]
-    for k in range(1, attn):
-        total = total + swap(outs[k], "attn", k).astype(f32)
+    outs, own, home = reduced(0)
+    total = outs[pair].astype(f32) + own
+    for came in home + from_sect:
+        total = total + came.astype(f32)
     return total.astype(bf16)
 
 

time: 75.4 us -> 68.8 us (0.912)
  waiting for transfers between devices: 44.3 us -> 24.9 us
  starting transfers between devices: 23.8 us -> 36.4 us
    ppermute x10 -> x15, waiting for transfers between devices: 18.9 us -> 4.53 us  [rotate(): lax.ppermute(value, axis, [(i, (i + step) % size) for i in range(size)])]
    ppermute x12 -> x18, starting transfers between devices: 18.2 us -> 27.7 us  [swap(): return lax.ppermute(value, axis, [(i, i ^ mask) for i in range(size)])]
    ppermute x12 -> x18, waiting for transfers between devices: 25.4 us -> 20.3 us  [swap(): return lax.ppermute(value, axis, [(i, i ^ mask) for i in range(size)])]
    ppermute x10 -> x15, starting transfers between devices: 5.63 us -> 8.71 us  [rotate(): lax.ppermute(value, axis, [(i, (i + step) % size) for i in range(size)])]
    pallas_call x9 -> x11, Pallas kernels: 4.9 us -> 4.85 us  [call(): pl.pallas_call(kernel, out_shape=outs, in_specs=[VMEM] * len(operands), o...]
  transfers between devices with their start and end apart: 22 -> 33, of which waited for: 11 -> 13; matrix products, arithmetic and copies ran while one was open for 0% -> 0% of each run, Pallas kernels for 4% -> 7%
where the time goes in v1:
time: 68.8 us; the launch traced here: 68.7 us
  starting transfers between devices  36.4 us (53%)
  waiting for transfers between devices  24.9 us (36%)
  Pallas kernels  4.85 us (7%)
  between operations  0.99 us (1%)
  local copies, waits for them, and re-layouts  0.84 us (1%)
  other arithmetic  0.69 us (1%)
    ppermute x18, starting transfers between devices, swap(): return lax.ppermute(value, axis, [(i, i ^ mask) for i in range(size)])  27.7 us
    ppermute x18, waiting for transfers between devices, swap(): return lax.ppermute(value, axis, [(i, i ^ mask) for i in range(size)])  20.3 us
    ppermute x15, starting transfers between devices, rotate(): lax.ppermute(value, axis, [(i, (i + step) % size) for i in range(size)])  8.71 us
    pallas_call x11, Pallas kernels, call(): pl.pallas_call(kernel, out_shape=outs, in_specs=[VMEM] * len(operands), o...  4.85 us
    ppermute x15, waiting for transfers between devices, rotate(): lax.ppermute(value, axis, [(i, (i + step) % size) for i in range(size)])  4.53 us
  transfers between devices with their start and end apart: 33, of which 13 were waited for; matrix products, arithmetic and copies ran while one was open for 0% of the time, Pallas kernels for 7%

profile of v1, /device:TPU:0, one launch (start us, length us, event | category | flops | bytes accessed | tf_op | source)
XLA Modules:
  0.0 68.7 jit_solution(14586507522099479207)
XLA Ops:
  1.8 4.1 %collective-permute-start.1 = (bf16[64,1024]{1,0:T(8,128)(2,1)S(1)}, bf16[64,1024]{1,0:T(8,128)(2,1)S(1)}, u32[]{:S(2)}, u32[]{:S(2)}) collective-permute-start(bf16[64,1024]{1,0:T(8,128)(2,1)S(1)} %get-tuple-element.35.refs_0_), channel_id=1, source_target_pairs={{0,8},{4,12},{8,0},{12,4},{1,9},{5,13},{9,1},{13,5},{2,10},{6,14},... | collective-permute-start | bytes 393224 | tf_op jit(solution)/shard_map/ppermute | solution.py:123
  5.9 1.5 %collective-permute-start.15 = (bf16[384,1024]{1,0:T(8,128)(2,1)S(1)}, bf16[384,1024]{1,0:T(8,128)(2,1)S(1)}, u32[]{:S(2)}, u32[]{:S(2)}) collective-permute-start(bf16[384,1024]{1,0:T(8,128)(2,1)S(1)} %get-tuple-element.48), channel_id=1, source_target_pairs={{0,2},{2,0},{1,3},{3,1},{4,6},{6,4},{5,7},{7,5},{8,10},{10,8},{9,1... | collective-permute-start | bytes 2359304 | tf_op jit(solution)/shard_map/ppermute | solution.py:118
  7.8 1.6 %collective-permute-start = (bf16[64,1024]{1,0:T(8,128)(2,1)S(1)}, bf16[64,1024]{1,0:T(8,128)(2,1)S(1)}, u32[]{:S(2)}, u32[]{:S(2)}) collective-permute-start(bf16[64,1024]{1,0:T(8,128)(2,1)S(1)} %get-tuple-element.35.refs_0_), channel_id=1, source_target_pairs={{0,4},{4,0},{8,12},{12,8},{1,5},{5,1},{9,13},{13,9},{2,6},{6,2},{1... | collective-permute-start | bytes 393224 | tf_op jit(solution)/shard_map/ppermute | solution.py:123
  9.3 6.0 %collective-permute-done.1.refs_2_ = bf16[64,1024]{1,0:T(8,128)(2,1)S(1)} collective-permute-done((bf16[64,1024]{1,0:T(8,128)(2,1)S(1)}, bf16[64,1024]{1,0:T(8,128)(2,1)S(1)}, u32[]{:S(2)}, u32[]{:S(2)}) %collective-permute-start.1) | collective-permute-done | bytes 131104 | tf_op jit(solution)/shard_map/ppermute | solution.py:123
  15.4 2.0 %collective-permute-start.3 = (bf16[176,256]{1,0:T(8,128)(2,1)S(1)}, bf16[176,256]{1,0:T(8,128)(2,1)S(1)}, u32[]{:S(2)}, u32[]{:S(2)}) collective-permute-start(bf16[176,256]{1,0:T(8,128)(2,1)S(1)} %get-tuple-element.37), channel_id=1, source_target_pairs={{0,4},{4,0},{8,12},{12,8},{1,5},{5,1},{9,13},{13,9},{2,6},{6,2},{1... | collective-permute-start | bytes 270344 | tf_op jit(solution)/shard_map/ppermute | solution.py:123
  17.7 4.8 %collective-permute-done.3.refs_5_ = bf16[176,256]{1,0:T(8,128)(2,1)S(1)} collective-permute-done((bf16[176,256]{1,0:T(8,128)(2,1)S(1)}, bf16[176,256]{1,0:T(8,128)(2,1)S(1)}, u32[]{:S(2)}, u32[]{:S(2)}) %collective-permute-start.3) | collective-permute-done | bytes 90144 | tf_op jit(solution)/shard_map/ppermute | solution.py:123
  23.5 1.6 %shard_map.120 = (f32[128,512]{1,0:T(8,128)S(1)}, f32[128,512]{1,0:T(8,128)S(1)}, bf16[16,512]{1,0:T(8,128)(2,1)S(1)}) custom-call(bf16[64,1024]{1,0:T(8,128)(2,1)S(1)} %get-tuple-element.35.refs_0_, bf16[64,1024]{1,0:T(8,128)(2,1)S(1)} %collective-permute-done.refs_1_, bf16[64,1024]{1,0:T(8,128)(2,1)S(1)} %collective-permute-done.1.refs_2_, ...), custom_call_target="tpu_custom_call" | custom-call | flops 1048576 | bytes 1949696 | tf_op jit(solution)/shard_map/pallas_call | solution.py:390
  25.1 1.5 %collective-permute-done.6.refs_0_ = f32[128,512]{1,0:T(8,128)S(1)} collective-permute-done((f32[128,512]{1,0:T(8,128)S(1)}, f32[128,512]{1,0:T(8,128)S(1)}, u32[]{:S(2)}, u32[]{:S(2)}) %collective-permute-start.6) | collective-permute-done | bytes 262176 | tf_op jit(solution)/shard_map/ppermute | solution.py:118
  26.7 1.6 %collective-permute-start.7 = (bf16[64,512]{1,0:T(8,128)(2,1)S(1)}, bf16[64,512]{1,0:T(8,128)(2,1)S(1)}, u32[]{:S(2)}, u32[]{:S(2)}) collective-permute-start(bf16[64,512]{1,0:T(8,128)(2,1)S(1)} %get-tuple-element.44), channel_id=1, source_target_pairs={{0,2},{2,0},{1,3},{3,1},{4,6},{6,4},{5,7},{7,5},{8,10},{10,8},{9,1... | collective-permute-start | bytes 196616 | tf_op jit(solution)/shard_map/ppermute | solution.py:118
  28.8 2.5 %collective-permute-done.7.refs_0_ = bf16[64,512]{1,0:T(8,128)(2,1)S(1)} collective-permute-done((bf16[64,512]{1,0:T(8,128)(2,1)S(1)}, bf16[64,512]{1,0:T(8,128)(2,1)S(1)}, u32[]{:S(2)}, u32[]{:S(2)}) %collective-permute-start.7) | collective-permute-done | bytes 65568 | tf_op jit(solution)/shard_map/ppermute | solution.py:118
  31.3 1.3 %collective-permute-start.8 = (bf16[64,512]{1,0:T(8,128)(2,1)S(1)}, bf16[64,512]{1,0:T(8,128)(2,1)S(1)}, u32[]{:S(2)}, u32[]{:S(2)}) collective-permute-start(bf16[64,512]{1,0:T(8,128)(2,1)S(1)} %get-tuple-element.46), channel_id=1, source_target_pairs={{0,4},{4,0},{8,12},{12,8},{1,5},{5,1},{9,13},{13,9},{2,6},{6,2},{1... | collective-permute-start | bytes 196616 | tf_op jit(solution)/shard_map/ppermute | solution.py:123
  32.6 3.9 %collective-permute-start.9 = (bf16[64,512]{1,0:T(8,128)(2,1)S(1)}, bf16[64,512]{1,0:T(8,128)(2,1)S(1)}, u32[]{:S(2)}, u32[]{:S(2)}) collective-permute-start(bf16[64,512]{1,0:T(8,128)(2,1)S(1)} %get-tuple-element.46), channel_id=1, source_target_pairs={{0,8},{4,12},{8,0},{12,4},{1,9},{5,13},{9,1},{13,5},{2,10},{6,14},... | collective-permute-start | bytes 196616 | tf_op jit(solution)/shard_map/ppermute | solution.py:123
  37.2 3.8 %collective-permute-start.22 = (bf16[64,512]{1,0:T(8,128)(2,1)S(1)}, bf16[64,512]{1,0:T(8,128)(2,1)S(1)}, u32[]{:S(2)}, u32[]{:S(2)}) collective-permute-start(bf16[64,512]{1,0:T(8,128)(2,1)S(1)} %get-tuple-element.58), channel_id=1, source_target_pairs={{0,8},{4,12},{8,0},{12,4},{1,9},{5,13},{9,1},{13,5},{2,10},{6,14},... | collective-permute-start | bytes 196616 | tf_op jit(solution)/shard_map/ppermute | solution.py:123
  43.4 2.3 %collective-permute-done.22.refs_2_ = bf16[64,512]{1,0:T(8,128)(2,1)S(1)} collective-permute-done((bf16[64,512]{1,0:T(8,128)(2,1)S(1)}, bf16[64,512]{1,0:T(8,128)(2,1)S(1)}, u32[]{:S(2)}, u32[]{:S(2)}) %collective-permute-start.22) | collective-permute-done | bytes 65568 | tf_op jit(solution)/shard_map/ppermute | solution.py:123
  45.8 1.6 %collective-permute-done.23.refs_3_ = bf16[64,512]{1,0:T(8,128)(2,1)S(1)} collective-permute-done((bf16[64,512]{1,0:T(8,128)(2,1)S(1)}, bf16[64,512]{1,0:T(8,128)(2,1)S(1)}, u32[]{:S(2)}, u32[]{:S(2)}) %collective-permute-start.23) | collective-permute-done | bytes 65568 | tf_op jit(solution)/shard_map/ppermute | solution.py:123
  48.8 1.5 %shard_map.126 = (f32[64,2048]{1,0:T(8,128)S(1)}, bf16[64,2048]{1,0:T(8,128)(2,1)S(1)}) custom-call(bf16[80,512]{1,0:T(8,128)(2,1)S(1)} %get-tuple-element.57.refs_0_, bf16[64,512]{1,0:T(8,128)(2,1)S(1)} %collective-permute-done.21.refs_1_, bf16[64,512]{1,0:T(8,128)(2,1)S(1)} %collective-permute-done.22.refs_2_, ...), custom_call_target="tpu_custom_call" | custom-call | flops 2147483648 | bytes 5316608 | tf_op jit(solution)/shard_map/pallas_call | solution.py:390
  50.7 1.5 %shard_map.123 = (f32[64,2048]{1,0:T(8,128)S(1)}, bf16[64,2048]{1,0:T(8,128)(2,1)S(1)}, bf16[16,2048]{1,0:T(8,128)(2,1)S(1)}) custom-call(bf16[80,512]{1,0:T(8,128)(2,1)S(1)} %get-tuple-element.45.refs_0_, bf16[64,512]{1,0:T(8,128)(2,1)S(1)} %collective-permute-done.8.refs_1_, bf16[64,512]{1,0:T(8,128)(2,1)S(1)} %collective-permute-done.9.refs_2_, ...), custom_call_target="tpu_custom_call" | custom-call | flops 2147483648 | bytes 5316608 | tf_op jit(solution)/shard_map/pallas_call | solution.py:390
  52.6 2.0 %collective-permute-start.30 = (bf16[16,2048]{1,0:T(8,128)(2,1)S(1)}, bf16[16,2048]{1,0:T(8,128)(2,1)S(1)}, u32[]{:S(2)}, u32[]{:S(2)}) collective-permute-start(bf16[16,2048]{1,0:T(8,128)(2,1)S(1)} %get-tuple-element.63), channel_id=1, source_target_pairs={{0,8},{4,12},{8,0},{12,4},{1,9},{5,13},{9,1},{13,5},{2,10},{6,14},... | collective-permute-start | bytes 196616 | tf_op jit(solution)/shard_map/ppermute | solution.py:123
  54.6 2.4 %collective-permute-start.31 = (bf16[16,2048]{1,0:T(8,128)(2,1)S(1)}, bf16[16,2048]{1,0:T(8,128)(2,1)S(1)}, u32[]{:S(2)}, u32[]{:S(2)}) collective-permute-start(bf16[16,2048]{1,0:T(8,128)(2,1)S(1)} %get-tuple-element.64), channel_id=1, source_target_pairs={{0,12},{4,8},{8,4},{12,0},{1,13},{5,9},{9,5},{13,1},{2,14},{6,10},... | collective-permute-start | bytes 196616 | tf_op jit(solution)/shard_map/ppermute | solution.py:123
  57.0 1.5 %collective-permute-start.19 = (bf16[16,2048]{1,0:T(8,128)(2,1)S(1)}, bf16[16,2048]{1,0:T(8,128)(2,1)S(1)}, u32[]{:S(2)}, u32[]{:S(2)}) collective-permute-start(bf16[16,2048]{1,0:T(8,128)(2,1)S(1)} %get-tuple-element.55), channel_id=1, source_target_pairs={{0,12},{4,8},{8,4},{12,0},{1,13},{5,9},{9,5},{13,1},{2,14},{6,10},... | collective-permute-start | bytes 196616 | tf_op jit(solution)/shard_map/ppermute | solution.py:123
  58.5 2.9 %collective-permute-start.17 = (bf16[16,2048]{1,0:T(8,128)(2,1)S(1)}, bf16[16,2048]{1,0:T(8,128)(2,1)S(1)}, u32[]{:S(2)}, u32[]{:S(2)}) collective-permute-start(bf16[16,2048]{1,0:T(8,128)(2,1)S(1)} %get-tuple-element.53), channel_id=1, source_target_pairs={{0,4},{4,0},{8,12},{12,8},{1,5},{5,1},{9,13},{13,9},{2,6},{6,2},{1... | collective-permute-start | bytes 196616 | tf_op jit(solution)/shard_map/ppermute | solution.py:123
  61.5 1.5 %collective-permute-done.30.refs_1_ = bf16[16,2048]{1,0:T(8,128)(2,1)S(1)} collective-permute-done((bf16[16,2048]{1,0:T(8,128)(2,1)S(1)}, bf16[16,2048]{1,0:T(8,128)(2,1)S(1)}, u32[]{:S(2)}, u32[]{:S(2)}) %collective-permute-start.30) | collective-permute-done | bytes 65568 | tf_op jit(solution)/shard_map/ppermute | solution.py:123
  63.0 2.7 %collective-permute-start.32 = (bf16[16,2048]{1,0:T(8,128)(2,1)S(1)}, bf16[16,2048]{1,0:T(8,128)(2,1)S(1)}, u32[]{:S(2)}, u32[]{:S(2)}) collective-permute-start(bf16[16,2048]{1,0:T(8,128)(2,1)S(1)} %shard_map.128), channel_id=1, source_target_pairs={{0,2},{2,0},{1,3},{3,1},{4,6},{6,4},{5,7},{7,5},{8,10},{10,8},{9,1... | collective-permute-start | bytes 196616 | tf_op jit(solution)/shard_map/ppermute | solution.py:118
  65.7 2.0 %collective-permute-done.18 = bf16[16,2048]{1,0:T(8,128)(2,1)S(1)} collective-permute-done((bf16[16,2048]{1,0:T(8,128)(2,1)S(1)}, bf16[16,2048]{1,0:T(8,128)(2,1)S(1)}, u32[]{:S(2)}, u32[]{:S(2)}) %collective-permute-start.18) | collective-permute-done | bytes 65568 | tf_op jit(solution)/shard_map/ppermute | solution.py:123
  (77 shorter events, 9.4 us)
Async XLA Ops:
  1.8 13.6 %collective-permute-start.1 = (bf16[64,1024]{1,0:T(8,128)(2,1)S(1)}, bf16[64,1024]{1,0:T(8,128)(2,1)S(1)}, u32[]{:S(2)}, u32[]{:S(2)}) collective-permute-start(bf16[64,1024]{1,0:T(8,128)(2,1)S(1)} %get-tuple-element.35.refs_0_), channel_id=1, source_target_pairs={{0,8},{4,12},{8,0},{12,4},{1,9},{5,13},{9,1},{13,5},{2,10},{6,14},... | collective-permute-start | bytes 393224 | tf_op jit(solution)/shard_map/ppermute | solution.py:123
  5.9 42.9 %collective-permute-start.15 = (bf16[384,1024]{1,0:T(8,128)(2,1)S(1)}, bf16[384,1024]{1,0:T(8,128)(2,1)S(1)}, u32[]{:S(2)}, u32[]{:S(2)}) collective-permute-start(bf16[384,1024]{1,0:T(8,128)(2,1)S(1)} %get-tuple-element.48), channel_id=1, source_target_pairs={{0,2},{2,0},{1,3},{3,1},{4,6},{6,4},{5,7},{7,5},{8,10},{10,8},{9,1... | collective-permute-start | bytes 2359304 | tf_op jit(solution)/shard_map/ppermute | solution.py:118
  7.4 10.0 %collective-permute-start.4 = (bf16[208,256]{1,0:T(8,128)(2,1)S(1)}, bf16[208,256]{1,0:T(8,128)(2,1)S(1)}, u32[]{:S(2)}, u32[]{:S(2)}) collective-permute-start(bf16[208,256]{1,0:T(8,128)(2,1)S(1)} %get-tuple-element.38), channel_id=1, source_target_pairs={{0,8},{4,12},{8,0},{12,4},{1,9},{5,13},{9,1},{13,5},{2,10},{6,14},... | collective-permute-start | bytes 319496 | tf_op jit(solution)/shard_map/ppermute | solution.py:123
  7.8 14.8 %collective-permute-start = (bf16[64,1024]{1,0:T(8,128)(2,1)S(1)}, bf16[64,1024]{1,0:T(8,128)(2,1)S(1)}, u32[]{:S(2)}, u32[]{:S(2)}) collective-permute-start(bf16[64,1024]{1,0:T(8,128)(2,1)S(1)} %get-tuple-element.35.refs_0_), channel_id=1, source_target_pairs={{0,4},{4,0},{8,12},{12,8},{1,5},{5,1},{9,13},{13,9},{2,6},{6,2},{1... | collective-permute-start | bytes 393224 | tf_op jit(solution)/shard_map/ppermute | solution.py:123
  15.4 8.1 %collective-permute-start.2 = (bf16[64,1024]{1,0:T(8,128)(2,1)S(1)}, bf16[64,1024]{1,0:T(8,128)(2,1)S(1)}, u32[]{:S(2)}, u32[]{:S(2)}) collective-permute-start(bf16[64,1024]{1,0:T(8,128)(2,1)S(1)} %collective-permute-done.1.refs_2_), channel_id=1, source_target_pairs={{0,4},{4,0},{8,12},{12,8},{1,5},{5,1},{9,13},{13,9},{2,6},{6,2},{1... | collective-permute-start | bytes 393224 | tf_op jit(solution)/shard_map/ppermute | solution.py:123
  15.4 7.1 %collective-permute-start.3 = (bf16[176,256]{1,0:T(8,128)(2,1)S(1)}, bf16[176,256]{1,0:T(8,128)(2,1)S(1)}, u32[]{:S(2)}, u32[]{:S(2)}) collective-permute-start(bf16[176,256]{1,0:T(8,128)(2,1)S(1)} %get-tuple-element.37), channel_id=1, source_target_pairs={{0,4},{4,0},{8,12},{12,8},{1,5},{5,1},{9,13},{13,9},{2,6},{6,2},{1... | collective-permute-start | bytes 270344 | tf_op jit(solution)/shard_map/ppermute | solution.py:123
  17.4 6.0 %collective-permute-start.5 = (bf16[176,256]{1,0:T(8,128)(2,1)S(1)}, bf16[176,256]{1,0:T(8,128)(2,1)S(1)}, u32[]{:S(2)}, u32[]{:S(2)}) collective-permute-start(bf16[176,256]{1,0:T(8,128)(2,1)S(1)} %slice.4), channel_id=1, source_target_pairs={{0,4},{4,0},{8,12},{12,8},{1,5},{5,1},{9,13},{13,9},{2,6},{6,2},{1... | collective-permute-start | bytes 270344 | tf_op jit(solution)/shard_map/ppermute | solution.py:123
  26.7 4.6 %collective-permute-start.7 = (bf16[64,512]{1,0:T(8,128)(2,1)S(1)}, bf16[64,512]{1,0:T(8,128)(2,1)S(1)}, u32[]{:S(2)}, u32[]{:S(2)}) collective-permute-start(bf16[64,512]{1,0:T(8,128)(2,1)S(1)} %get-tuple-element.44), channel_id=1, source_target_pairs={{0,2},{2,0},{1,3},{3,1},{4,6},{6,4},{5,7},{7,5},{8,10},{10,8},{9,1... | collective-permute-start | bytes 196616 | tf_op jit(solution)/shard_map/ppermute | solution.py:118
  28.3 8.2 %collective-permute-start.20 = (bf16[80,512]{1,0:T(8,128)(2,1)S(1)}, bf16[80,512]{1,0:T(8,128)(2,1)S(1)}, u32[]{:S(2)}, u32[]{:S(2)}) collective-permute-start(bf16[80,512]{1,0:T(8,128)(2,1)S(1)} %get-tuple-element.43.names_ref), channel_id=1, source_target_pairs={{0,2},{2,0},{1,3},{3,1},{4,6},{6,4},{5,7},{7,5},{8,10},{10,8},{9,1... | collective-permute-start | bytes 245768 | tf_op jit(solution)/shard_map/ppermute | solution.py:118
  31.3 5.9 %collective-permute-start.8 = (bf16[64,512]{1,0:T(8,128)(2,1)S(1)}, bf16[64,512]{1,0:T(8,128)(2,1)S(1)}, u32[]{:S(2)}, u32[]{:S(2)}) collective-permute-start(bf16[64,512]{1,0:T(8,128)(2,1)S(1)} %get-tuple-element.46), channel_id=1, source_target_pairs={{0,4},{4,0},{8,12},{12,8},{1,5},{5,1},{9,13},{13,9},{2,6},{6,2},{1... | collective-permute-start | bytes 196616 | tf_op jit(solution)/shard_map/ppermute | solution.py:123
  32.6 8.8 %collective-permute-start.9 = (bf16[64,512]{1,0:T(8,128)(2,1)S(1)}, bf16[64,512]{1,0:T(8,128)(2,1)S(1)}, u32[]{:S(2)}, u32[]{:S(2)}) collective-permute-start(bf16[64,512]{1,0:T(8,128)(2,1)S(1)} %get-tuple-element.46), channel_id=1, source_target_pairs={{0,8},{4,12},{8,0},{12,4},{1,9},{5,13},{9,1},{13,5},{2,10},{6,14},... | collective-permute-start | bytes 196616 | tf_op jit(solution)/shard_map/ppermute | solution.py:123
  36.5 6.4 %collective-permute-start.10 = (bf16[64,512]{1,0:T(8,128)(2,1)S(1)}, bf16[64,512]{1,0:T(8,128)(2,1)S(1)}, u32[]{:S(2)}, u32[]{:S(2)}) collective-permute-start(bf16[64,512]{1,0:T(8,128)(2,1)S(1)} %get-tuple-element.46), channel_id=1, source_target_pairs={{0,12},{4,8},{8,4},{12,0},{1,13},{5,9},{9,5},{13,1},{2,14},{6,10},... | collective-permute-start | bytes 196616 | tf_op jit(solution)/shard_map/ppermute | solution.py:123
  36.5 6.4 %collective-permute-start.21 = (bf16[64,512]{1,0:T(8,128)(2,1)S(1)}, bf16[64,512]{1,0:T(8,128)(2,1)S(1)}, u32[]{:S(2)}, u32[]{:S(2)}) collective-permute-start(bf16[64,512]{1,0:T(8,128)(2,1)S(1)} %get-tuple-element.58), channel_id=1, source_target_pairs={{0,4},{4,0},{8,12},{12,8},{1,5},{5,1},{9,13},{13,9},{2,6},{6,2},{1... | collective-permute-start | bytes 196616 | tf_op jit(solution)/shard_map/ppermute | solution.py:123
  37.2 8.6 %collective-permute-start.22 = (bf16[64,512]{1,0:T(8,128)(2,1)S(1)}, bf16[64,512]{1,0:T(8,128)(2,1)S(1)}, u32[]{:S(2)}, u32[]{:S(2)}) collective-permute-start(bf16[64,512]{1,0:T(8,128)(2,1)S(1)} %get-tuple-element.58), channel_id=1, source_target_pairs={{0,8},{4,12},{8,0},{12,4},{1,9},{5,13},{9,1},{13,5},{2,10},{6,14},... | collective-permute-start | bytes 196616 | tf_op jit(solution)/shard_map/ppermute | solution.py:123
  41.3 6.1 %collective-permute-start.23 = (bf16[64,512]{1,0:T(8,128)(2,1)S(1)}, bf16[64,512]{1,0:T(8,128)(2,1)S(1)}, u32[]{:S(2)}, u32[]{:S(2)}) collective-permute-start(bf16[64,512]{1,0:T(8,128)(2,1)S(1)} %get-tuple-element.58), channel_id=1, source_target_pairs={{0,12},{4,8},{8,4},{12,0},{1,13},{5,9},{9,5},{13,1},{2,14},{6,10},... | collective-permute-start | bytes 196616 | tf_op jit(solution)/shard_map/ppermute | solution.py:123
  42.9 5.0 %collective-permute-start.25 = (bf16[64,512]{1,0:T(8,128)(2,1)S(1)}, bf16[64,512]{1,0:T(8,128)(2,1)S(1)}, u32[]{:S(2)}, u32[]{:S(2)}) collective-permute-start(bf16[64,512]{1,0:T(8,128)(2,1)S(1)} %collective-permute-done.21.refs_1_), channel_id=1, source_target_pairs={{0,1},{1,0},{2,3},{3,2},{4,5},{5,4},{6,7},{7,6},{8,9},{9,8},{10,11... | collective-permute-start | bytes 196616 | tf_op jit(solution)/shard_map/ppermute | solution.py:118
  52.2 4.7 %collective-permute-start.16 = (bf16[64,2048]{1,0:T(8,128)(2,1)S(1)}, bf16[64,2048]{1,0:T(8,128)(2,1)S(1)}, u32[]{:S(2)}, u32[]{:S(2)}) collective-permute-start(bf16[64,2048]{1,0:T(8,128)(2,1)S(1)} %get-tuple-element.51), channel_id=1, source_target_pairs={{0,1},{1,0},{2,3},{3,2},{4,5},{5,4},{6,7},{7,6},{8,9},{9,8},{10,11... | collective-permute-start | bytes 786440 | tf_op jit(solution)/shard_map/ppermute | solution.py:118
  52.5 6.0 %collective-permute-start.29 = (bf16[16,2048]{1,0:T(8,128)(2,1)S(1)}, bf16[16,2048]{1,0:T(8,128)(2,1)S(1)}, u32[]{:S(2)}, u32[]{:S(2)}) collective-permute-start(bf16[16,2048]{1,0:T(8,128)(2,1)S(1)} %get-tuple-element.62), channel_id=1, source_target_pairs={{0,4},{4,0},{8,12},{12,8},{1,5},{5,1},{9,13},{13,9},{2,6},{6,2},{1... | collective-permute-start | bytes 196616 | tf_op jit(solution)/shard_map/ppermute | solution.py:123
  52.6 10.4 %collective-permute-start.30 = (bf16[16,2048]{1,0:T(8,128)(2,1)S(1)}, bf16[16,2048]{1,0:T(8,128)(2,1)S(1)}, u32[]{:S(2)}, u32[]{:S(2)}) collective-permute-start(bf16[16,2048]{1,0:T(8,128)(2,1)S(1)} %get-tuple-element.63), channel_id=1, source_target_pairs={{0,8},{4,12},{8,0},{12,4},{1,9},{5,13},{9,1},{13,5},{2,10},{6,14},... | collective-permute-start | bytes 196616 | tf_op jit(solution)/shard_map/ppermute | solution.py:123
  54.6 8.4 %collective-permute-start.31 = (bf16[16,2048]{1,0:T(8,128)(2,1)S(1)}, bf16[16,2048]{1,0:T(8,128)(2,1)S(1)}, u32[]{:S(2)}, u32[]{:S(2)}) collective-permute-start(bf16[16,2048]{1,0:T(8,128)(2,1)S(1)} %get-tuple-element.64), channel_id=1, source_target_pairs={{0,12},{4,8},{8,4},{12,0},{1,13},{5,9},{9,5},{13,1},{2,14},{6,10},... | collective-permute-start | bytes 196616 | tf_op jit(solution)/shard_map/ppermute | solution.py:123
  57.0 8.7 %collective-permute-start.19 = (bf16[16,2048]{1,0:T(8,128)(2,1)S(1)}, bf16[16,2048]{1,0:T(8,128)(2,1)S(1)}, u32[]{:S(2)}, u32[]{:S(2)}) collective-permute-start(bf16[16,2048]{1,0:T(8,128)(2,1)S(1)} %get-tuple-element.55), channel_id=1, source_target_pairs={{0,12},{4,8},{8,4},{12,0},{1,13},{5,9},{9,5},{13,1},{2,14},{6,10},... | collective-permute-start | bytes 196616 | tf_op jit(solution)/shard_map/ppermute | solution.py:123
  58.5 9.2 %collective-permute-start.18 = (bf16[16,2048]{1,0:T(8,128)(2,1)S(1)}, bf16[16,2048]{1,0:T(8,128)(2,1)S(1)}, u32[]{:S(2)}, u32[]{:S(2)}) collective-permute-start(bf16[16,2048]{1,0:T(8,128)(2,1)S(1)} %get-tuple-element.54), channel_id=1, source_target_pairs={{0,8},{4,12},{8,0},{12,4},{1,9},{5,13},{9,1},{13,5},{2,10},{6,14},... | collective-permute-start | bytes 196616 | tf_op jit(solution)/shard_map/ppermute | solution.py:123
  58.5 9.2 %collective-permute-start.17 = (bf16[16,2048]{1,0:T(8,128)(2,1)S(1)}, bf16[16,2048]{1,0:T(8,128)(2,1)S(1)}, u32[]{:S(2)}, u32[]{:S(2)}) collective-permute-start(bf16[16,2048]{1,0:T(8,128)(2,1)S(1)} %get-tuple-element.53), channel_id=1, source_target_pairs={{0,4},{4,0},{8,12},{12,8},{1,5},{5,1},{9,13},{13,9},{2,6},{6,2},{1... | collective-permute-start | bytes 196616 | tf_op jit(solution)/shard_map/ppermute | solution.py:123
  63.0 5.0 %collective-permute-start.32 = (bf16[16,2048]{1,0:T(8,128)(2,1)S(1)}, bf16[16,2048]{1,0:T(8,128)(2,1)S(1)}, u32[]{:S(2)}, u32[]{:S(2)}) collective-permute-start(bf16[16,2048]{1,0:T(8,128)(2,1)S(1)} %shard_map.128), channel_id=1, source_target_pairs={{0,2},{2,0},{1,3},{3,1},{4,6},{6,4},{5,7},{7,5},{8,10},{10,8},{9,1... | collective-permute-start | bytes 196616 | tf_op jit(solution)/shard_map/ppermute | solution.py:118
  (20 other events, 178.1 us)

commit v2 on v1

--- a/solution.py
+++ b/solution.py
@@ -128,10 +128,9 @@
 
 
 def pack_kernel(attn, sect, *refs):
-    _, q_ref, kv_ref, list_ref, len_ref, res_ref, ids_ref, down_ref, *refs = refs
-    own_ref, far_ref, near_ref, q_out, *downs = refs
+    _, kv_ref, list_ref, len_ref, res_ref, ids_ref, down_ref, *refs = refs
+    own_ref, far_ref, near_ref, *downs = refs
     my_attn, my_sect = lax.axis_index("attn"), lax.axis_index("sect")
-    q_out[...] = q_ref[...]
     ff = downs[0].shape[0]
     for i in range(sect):
         start = pl.multiple_of(lax.rem(my_sect + i, sect) * ff, ff)
@@ -148,8 +147,9 @@
     list_len = list_ref.shape[1]
     for j in range(list_len):
         facts = jnp.where(lane == j, list_ref[:, j : j + 1], facts)
-    facts = jnp.where(lane == list_len, len_ref[...] // 128, facts)
-    facts = jnp.where(lane == list_len + 1, lax.rem(len_ref[...], 128), facts)
+    length = jnp.broadcast_to(len_ref[...], (per_dev, 1))
+    facts = jnp.where(lane == list_len, length // 128, facts)
+    facts = jnp.where(lane == list_len + 1, lax.rem(length, 128), facts)
     facts = facts.astype(jnp.float32).astype(jnp.bfloat16)
     eye = (
         lax.broadcasted_iota(jnp.int32, (per_dev, per_dev), 0)
@@ -427,14 +427,15 @@
     packed = slice_rows + blocks * keys + per_dev
 
     anchor = call(anchor_kernel, [], shape((8, 128), f32), flops=1 << 34)
-    own_pack, far_pack, near_pack, own_q, *downs = call(
+    far_q = swap(queries, "attn", 2)
+    near_q = swap(queries, "attn", 1)
+    own_pack, far_pack, near_pack, *downs = call(
         functools.partial(pack_kernel, attn, sect),
         [
             anchor,
-            queries,
             kv_pool,
             block_list,
-            cache_len.reshape(1, 1),
+            cache_len,
             residual,
             expert_ids.T,
             w_down[0],
@@ -443,18 +444,15 @@
             shape((packed, kv_cols), bf16),
             shape((packed + slice_rows, kv_cols), bf16),
             shape((packed, kv_cols), bf16),
-            shape(queries.shape, bf16),
         ]
         + [shape((ff, w_down.shape[2]), bf16)] * sect,
     )
     far_pack = swap(far_pack, "attn", 2)
-    far_q = swap(own_q, "attn", 2)
     downs = [downs[0]] + [rotate(downs[i], "sect", i) for i in range(1, sect)]
     near_pack = swap(near_pack, "attn", 1)
-    near_q = swap(own_q, "attn", 1)
     last_pack = swap(far_pack[slice_rows:], "attn", 1)
     last_q = swap(far_q, "attn", 1)
-    q = [own_q, near_q, far_q, last_q]
+    q = [queries, near_q, far_q, last_q]
     packs = [own_pack, near_pack, far_pack, last_pack]
 
     parts = call(

time: 68.8 us -> 67.6 us (0.983)
  local copies, waits for them, and re-layouts: 0.84 us -> 0.06 us
  waiting for transfers between devices: 24.9 us -> 24.2 us
    ppermute x18, waiting for transfers between devices: 20.3 us -> 19.5 us  [swap(): return lax.ppermute(value, axis, [(i, i ^ mask) for i in range(size)])]
    unnamed x22, local copies, waits for them, and re-layouts: 0.83 us -> 0.05 us
  transfers between devices with their start and end apart: 33 -> 33, of which waited for: 13 -> 12; matrix products, arithmetic and copies ran while one was open for 0% -> 0% of each run, Pallas kernels for 7% -> 7%
where the time goes in v2:
time: 67.6 us; the launch traced here: 67.5 us
  starting transfers between devices  36.7 us (54%)
  waiting for transfers between devices  24.2 us (36%)
  Pallas kernels  4.85 us (7%)
  between operations  0.95 us (1%)
  other arithmetic  0.69 us (1%)
    ppermute x18, starting transfers between devices, swap(): return lax.ppermute(value, axis, [(i, i ^ mask) for i in range(size)])  28.3 us
    ppermute x18, waiting for transfers between devices, swap(): return lax.ppermute(value, axis, [(i, i ^ mask) for i in range(size)])  19.5 us
    ppermute x15, starting transfers between devices, rotate(): lax.ppermute(value, axis, [(i, (i + step) % size) for i in range(size)])  8.38 us
    pallas_call x11, Pallas kernels, call(): pl.pallas_call(kernel, out_shape=outs, in_specs=[VMEM] * len(operands), o...  4.85 us
    ppermute x15, waiting for transfers between devices, rotate(): lax.ppermute(value, axis, [(i, (i + step) % size) for i in range(size)])  4.71 us
  transfers between devices with their start and end apart: 33, of which 12 were waited for; matrix products, arithmetic and copies ran while one was open for 0% of the time, Pallas kernels for 7%

profile of v2, /device:TPU:0, one launch (start us, length us, event | category | flops | bytes accessed | tf_op | source)
XLA Modules:
  0.0 67.5 jit_solution(2254345972108318771)
XLA Ops:
  0.0 4.1 %collective-permute-start.1 = (bf16[64,1024]{1,0:T(8,128)(2,1)}, bf16[64,1024]{1,0:T(8,128)(2,1)S(1)}, u32[]{:S(2)}, u32[]{:S(2)}) collective-permute-start(bf16[64,1024]{1,0:T(8,128)(2,1)} %refs_0_.1), channel_id=1, source_target_pairs={{0,8},{4,12},{8,0},{12,4},{1,9},{5,13},{9,1},{13,5},{2,10},{6,14},... | collective-permute-start | bytes 393224 | tf_op jit(solution)/shard_map/ppermute | solution.py:123
  5.1 1.6 %collective-permute-start.15 = (bf16[384,1024]{1,0:T(8,128)(2,1)S(1)}, bf16[384,1024]{1,0:T(8,128)(2,1)S(1)}, u32[]{:S(2)}, u32[]{:S(2)}) collective-permute-start(bf16[384,1024]{1,0:T(8,128)(2,1)S(1)} %get-tuple-element.46), channel_id=1, source_target_pairs={{0,2},{2,0},{1,3},{3,1},{4,6},{6,4},{5,7},{7,5},{8,10},{10,8},{9,1... | collective-permute-start | bytes 2359304 | tf_op jit(solution)/shard_map/ppermute | solution.py:118
  7.3 1.6 %collective-permute-start = (bf16[64,1024]{1,0:T(8,128)(2,1)S(1)}, bf16[64,1024]{1,0:T(8,128)(2,1)S(1)}, u32[]{:S(2)}, u32[]{:S(2)}) collective-permute-start(bf16[64,1024]{1,0:T(8,128)(2,1)S(1)} %copy-done.3), channel_id=1, source_target_pairs={{0,4},{4,0},{8,12},{12,8},{1,5},{5,1},{9,13},{13,9},{2,6},{6,2},{1... | collective-permute-start | bytes 393224 | tf_op jit(solution)/shard_map/ppermute | solution.py:123
  8.9 4.3 %collective-permute-done.1.refs_2_ = bf16[64,1024]{1,0:T(8,128)(2,1)S(1)} collective-permute-done((bf16[64,1024]{1,0:T(8,128)(2,1)}, bf16[64,1024]{1,0:T(8,128)(2,1)S(1)}, u32[]{:S(2)}, u32[]{:S(2)}) %collective-permute-start.1) | collective-permute-done | bytes 131104 | tf_op jit(solution)/shard_map/ppermute | solution.py:123
  13.9 1.3 %collective-permute-start.3 = (bf16[176,256]{1,0:T(8,128)(2,1)S(1)}, bf16[176,256]{1,0:T(8,128)(2,1)S(1)}, u32[]{:S(2)}, u32[]{:S(2)}) collective-permute-start(bf16[176,256]{1,0:T(8,128)(2,1)S(1)} %get-tuple-element.35), channel_id=1, source_target_pairs={{0,4},{4,0},{8,12},{12,8},{1,5},{5,1},{9,13},{13,9},{2,6},{6,2},{1... | collective-permute-start | bytes 270344 | tf_op jit(solution)/shard_map/ppermute | solution.py:123
  16.1 5.4 %collective-permute-done.3.refs_5_ = bf16[176,256]{1,0:T(8,128)(2,1)S(1)} collective-permute-done((bf16[176,256]{1,0:T(8,128)(2,1)S(1)}, bf16[176,256]{1,0:T(8,128)(2,1)S(1)}, u32[]{:S(2)}, u32[]{:S(2)}) %collective-permute-start.3) | collective-permute-done | bytes 90144 | tf_op jit(solution)/shard_map/ppermute | solution.py:123
  22.4 1.6 %shard_map.120 = (f32[128,512]{1,0:T(8,128)S(1)}, f32[128,512]{1,0:T(8,128)S(1)}, bf16[16,512]{1,0:T(8,128)(2,1)S(1)}) custom-call(bf16[64,1024]{1,0:T(8,128)(2,1)S(1)} %copy-done.3, bf16[64,1024]{1,0:T(8,128)(2,1)S(1)} %collective-permute-done.refs_1_, bf16[64,1024]{1,0:T(8,128)(2,1)S(1)} %collective-permute-done.1.refs_2_, ...), custom_call_target="tpu_custom_call" | custom-call | flops 1048576 | bytes 1949696 | tf_op jit(solution)/shard_map/pallas_call | solution.py:390
  24.1 1.5 %collective-permute-done.6.refs_0_ = f32[128,512]{1,0:T(8,128)S(1)} collective-permute-done((f32[128,512]{1,0:T(8,128)S(1)}, f32[128,512]{1,0:T(8,128)S(1)}, u32[]{:S(2)}, u32[]{:S(2)}) %collective-permute-start.6) | collective-permute-done | bytes 262176 | tf_op jit(solution)/shard_map/ppermute | solution.py:118
  25.7 1.1 %collective-permute-start.7 = (bf16[64,512]{1,0:T(8,128)(2,1)S(1)}, bf16[64,512]{1,0:T(8,128)(2,1)S(1)}, u32[]{:S(2)}, u32[]{:S(2)}) collective-permute-start(bf16[64,512]{1,0:T(8,128)(2,1)S(1)} %get-tuple-element.42), channel_id=1, source_target_pairs={{0,2},{2,0},{1,3},{3,1},{4,6},{6,4},{5,7},{7,5},{8,10},{10,8},{9,1... | collective-permute-start | bytes 196616 | tf_op jit(solution)/shard_map/ppermute | solution.py:118
  26.7 1.0 %collective-permute-start.20 = (bf16[80,512]{1,0:T(8,128)(2,1)S(1)}, bf16[80,512]{1,0:T(8,128)(2,1)S(1)}, u32[]{:S(2)}, u32[]{:S(2)}) collective-permute-start(bf16[80,512]{1,0:T(8,128)(2,1)S(1)} %get-tuple-element.41.names_ref), channel_id=1, source_target_pairs={{0,2},{2,0},{1,3},{3,1},{4,6},{6,4},{5,7},{7,5},{8,10},{10,8},{9,1... | collective-permute-start | bytes 245768 | tf_op jit(solution)/shard_map/ppermute | solution.py:118
  27.8 2.9 %collective-permute-done.7.refs_0_ = bf16[64,512]{1,0:T(8,128)(2,1)S(1)} collective-permute-done((bf16[64,512]{1,0:T(8,128)(2,1)S(1)}, bf16[64,512]{1,0:T(8,128)(2,1)S(1)}, u32[]{:S(2)}, u32[]{:S(2)}) %collective-permute-start.7) | collective-permute-done | bytes 65568 | tf_op jit(solution)/shard_map/ppermute | solution.py:118
  31.0 4.6 %collective-permute-start.9 = (bf16[64,512]{1,0:T(8,128)(2,1)S(1)}, bf16[64,512]{1,0:T(8,128)(2,1)S(1)}, u32[]{:S(2)}, u32[]{:S(2)}) collective-permute-start(bf16[64,512]{1,0:T(8,128)(2,1)S(1)} %get-tuple-element.44), channel_id=1, source_target_pairs={{0,8},{4,12},{8,0},{12,4},{1,9},{5,13},{9,1},{13,5},{2,10},{6,14},... | collective-permute-start | bytes 196616 | tf_op jit(solution)/shard_map/ppermute | solution.py:123
  36.2 3.8 %collective-permute-start.22 = (bf16[64,512]{1,0:T(8,128)(2,1)S(1)}, bf16[64,512]{1,0:T(8,128)(2,1)S(1)}, u32[]{:S(2)}, u32[]{:S(2)}) collective-permute-start(bf16[64,512]{1,0:T(8,128)(2,1)S(1)} %get-tuple-element.56), channel_id=1, source_target_pairs={{0,8},{4,12},{8,0},{12,4},{1,9},{5,13},{9,1},{13,5},{2,10},{6,14},... | collective-permute-start | bytes 196616 | tf_op jit(solution)/shard_map/ppermute | solution.py:123
  42.6 2.3 %collective-permute-done.22.refs_2_ = bf16[64,512]{1,0:T(8,128)(2,1)S(1)} collective-permute-done((bf16[64,512]{1,0:T(8,128)(2,1)S(1)}, bf16[64,512]{1,0:T(8,128)(2,1)S(1)}, u32[]{:S(2)}, u32[]{:S(2)}) %collective-permute-start.22) | collective-permute-done | bytes 65568 | tf_op jit(solution)/shard_map/ppermute | solution.py:123
  44.8 1.6 %collective-permute-done.23.refs_3_ = bf16[64,512]{1,0:T(8,128)(2,1)S(1)} collective-permute-done((bf16[64,512]{1,0:T(8,128)(2,1)S(1)}, bf16[64,512]{1,0:T(8,128)(2,1)S(1)}, u32[]{:S(2)}, u32[]{:S(2)}) %collective-permute-start.23) | collective-permute-done | bytes 65568 | tf_op jit(solution)/shard_map/ppermute | solution.py:123
  47.9 1.5 %shard_map.126 = (f32[64,2048]{1,0:T(8,128)S(1)}, bf16[64,2048]{1,0:T(8,128)(2,1)S(1)}) custom-call(bf16[80,512]{1,0:T(8,128)(2,1)S(1)} %get-tuple-element.55.refs_0_, bf16[64,512]{1,0:T(8,128)(2,1)S(1)} %collective-permute-done.21.refs_1_, bf16[64,512]{1,0:T(8,128)(2,1)S(1)} %collective-permute-done.22.refs_2_, ...), custom_call_target="tpu_custom_call" | custom-call | flops 2147483648 | bytes 5316608 | tf_op jit(solution)/shard_map/pallas_call | solution.py:390
  49.8 1.5 %shard_map.123 = (f32[64,2048]{1,0:T(8,128)S(1)}, bf16[64,2048]{1,0:T(8,128)(2,1)S(1)}, bf16[16,2048]{1,0:T(8,128)(2,1)S(1)}) custom-call(bf16[80,512]{1,0:T(8,128)(2,1)S(1)} %get-tuple-element.43.refs_0_, bf16[64,512]{1,0:T(8,128)(2,1)S(1)} %collective-permute-done.8.refs_1_, bf16[64,512]{1,0:T(8,128)(2,1)S(1)} %collective-permute-done.9.refs_2_, ...), custom_call_target="tpu_custom_call" | custom-call | flops 2147483648 | bytes 5316608 | tf_op jit(solution)/shard_map/pallas_call | solution.py:390
  51.6 2.0 %collective-permute-start.30 = (bf16[16,2048]{1,0:T(8,128)(2,1)S(1)}, bf16[16,2048]{1,0:T(8,128)(2,1)S(1)}, u32[]{:S(2)}, u32[]{:S(2)}) collective-permute-start(bf16[16,2048]{1,0:T(8,128)(2,1)S(1)} %get-tuple-element.61), channel_id=1, source_target_pairs={{0,8},{4,12},{8,0},{12,4},{1,9},{5,13},{9,1},{13,5},{2,10},{6,14},... | collective-permute-start | bytes 196616 | tf_op jit(solution)/shard_map/ppermute | solution.py:123
  53.6 2.4 %collective-permute-start.31 = (bf16[16,2048]{1,0:T(8,128)(2,1)S(1)}, bf16[16,2048]{1,0:T(8,128)(2,1)S(1)}, u32[]{:S(2)}, u32[]{:S(2)}) collective-permute-start(bf16[16,2048]{1,0:T(8,128)(2,1)S(1)} %get-tuple-element.62), channel_id=1, source_target_pairs={{0,12},{4,8},{8,4},{12,0},{1,13},{5,9},{9,5},{13,1},{2,14},{6,10},... | collective-permute-start | bytes 196616 | tf_op jit(solution)/shard_map/ppermute | solution.py:123
  56.1 1.5 %collective-permute-start.19 = (bf16[16,2048]{1,0:T(8,128)(2,1)S(1)}, bf16[16,2048]{1,0:T(8,128)(2,1)S(1)}, u32[]{:S(2)}, u32[]{:S(2)}) collective-permute-start(bf16[16,2048]{1,0:T(8,128)(2,1)S(1)} %get-tuple-element.53), channel_id=1, source_target_pairs={{0,12},{4,8},{8,4},{12,0},{1,13},{5,9},{9,5},{13,1},{2,14},{6,10},... | collective-permute-start | bytes 196616 | tf_op jit(solution)/shard_map/ppermute | solution.py:123
  57.6 2.9 %collective-permute-start.17 = (bf16[16,2048]{1,0:T(8,128)(2,1)S(1)}, bf16[16,2048]{1,0:T(8,128)(2,1)S(1)}, u32[]{:S(2)}, u32[]{:S(2)}) collective-permute-start(bf16[16,2048]{1,0:T(8,128)(2,1)S(1)} %get-tuple-element.51), channel_id=1, source_target_pairs={{0,4},{4,0},{8,12},{12,8},{1,5},{5,1},{9,13},{13,9},{2,6},{6,2},{1... | collective-permute-start | bytes 196616 | tf_op jit(solution)/shard_map/ppermute | solution.py:123
  60.5 1.5 %collective-permute-done.30.refs_1_ = bf16[16,2048]{1,0:T(8,128)(2,1)S(1)} collective-permute-done((bf16[16,2048]{1,0:T(8,128)(2,1)S(1)}, bf16[16,2048]{1,0:T(8,128)(2,1)S(1)}, u32[]{:S(2)}, u32[]{:S(2)}) %collective-permute-start.30) | collective-permute-done | bytes 65568 | tf_op jit(solution)/shard_map/ppermute | solution.py:123
  62.1 2.3 %collective-permute-start.32 = (bf16[16,2048]{1,0:T(8,128)(2,1)S(1)}, bf16[16,2048]{1,0:T(8,128)(2,1)S(1)}, u32[]{:S(2)}, u32[]{:S(2)}) collective-permute-start(bf16[16,2048]{1,0:T(8,128)(2,1)S(1)} %shard_map.128), channel_id=1, source_target_pairs={{0,2},{2,0},{1,3},{3,1},{4,6},{6,4},{5,7},{7,5},{8,10},{10,8},{9,1... | collective-permute-start | bytes 196616 | tf_op jit(solution)/shard_map/ppermute | solution.py:118
  64.4 2.4 %collective-permute-done.18 = bf16[16,2048]{1,0:T(8,128)(2,1)S(1)} collective-permute-done((bf16[16,2048]{1,0:T(8,128)(2,1)S(1)}, bf16[16,2048]{1,0:T(8,128)(2,1)S(1)}, u32[]{:S(2)}, u32[]{:S(2)}) %collective-permute-start.18) | collective-permute-done | bytes 65568 | tf_op jit(solution)/shard_map/ppermute | solution.py:123
  (77 shorter events, 9.8 us)
Async XLA Ops:
  0.0 13.2 %collective-permute-start.1 = (bf16[64,1024]{1,0:T(8,128)(2,1)}, bf16[64,1024]{1,0:T(8,128)(2,1)S(1)}, u32[]{:S(2)}, u32[]{:S(2)}) collective-permute-start(bf16[64,1024]{1,0:T(8,128)(2,1)} %refs_0_.1), channel_id=1, source_target_pairs={{0,8},{4,12},{8,0},{12,4},{1,9},{5,13},{9,1},{13,5},{2,10},{6,14},... | collective-permute-start | bytes 393224 | tf_op jit(solution)/shard_map/ppermute | solution.py:123
  5.1 42.8 %collective-permute-start.15 = (bf16[384,1024]{1,0:T(8,128)(2,1)S(1)}, bf16[384,1024]{1,0:T(8,128)(2,1)S(1)}, u32[]{:S(2)}, u32[]{:S(2)}) collective-permute-start(bf16[384,1024]{1,0:T(8,128)(2,1)S(1)} %get-tuple-element.46), channel_id=1, source_target_pairs={{0,2},{2,0},{1,3},{3,1},{4,6},{6,4},{5,7},{7,5},{8,10},{10,8},{9,1... | collective-permute-start | bytes 2359304 | tf_op jit(solution)/shard_map/ppermute | solution.py:118
  6.7 8.6 %collective-permute-start.4 = (bf16[208,256]{1,0:T(8,128)(2,1)S(1)}, bf16[208,256]{1,0:T(8,128)(2,1)S(1)}, u32[]{:S(2)}, u32[]{:S(2)}) collective-permute-start(bf16[208,256]{1,0:T(8,128)(2,1)S(1)} %get-tuple-element.36), channel_id=1, source_target_pairs={{0,8},{4,12},{8,0},{12,4},{1,9},{5,13},{9,1},{13,5},{2,10},{6,14},... | collective-permute-start | bytes 319496 | tf_op jit(solution)/shard_map/ppermute | solution.py:123
  7.3 14.2 %collective-permute-start = (bf16[64,1024]{1,0:T(8,128)(2,1)S(1)}, bf16[64,1024]{1,0:T(8,128)(2,1)S(1)}, u32[]{:S(2)}, u32[]{:S(2)}) collective-permute-start(bf16[64,1024]{1,0:T(8,128)(2,1)S(1)} %copy-done.3), channel_id=1, source_target_pairs={{0,4},{4,0},{8,12},{12,8},{1,5},{5,1},{9,13},{13,9},{2,6},{6,2},{1... | collective-permute-start | bytes 393224 | tf_op jit(solution)/shard_map/ppermute | solution.py:123
  13.2 9.3 %collective-permute-start.2 = (bf16[64,1024]{1,0:T(8,128)(2,1)S(1)}, bf16[64,1024]{1,0:T(8,128)(2,1)S(1)}, u32[]{:S(2)}, u32[]{:S(2)}) collective-permute-start(bf16[64,1024]{1,0:T(8,128)(2,1)S(1)} %collective-permute-done.1.refs_2_), channel_id=1, source_target_pairs={{0,4},{4,0},{8,12},{12,8},{1,5},{5,1},{9,13},{13,9},{2,6},{6,2},{1... | collective-permute-start | bytes 393224 | tf_op jit(solution)/shard_map/ppermute | solution.py:123
  13.9 7.6 %collective-permute-start.3 = (bf16[176,256]{1,0:T(8,128)(2,1)S(1)}, bf16[176,256]{1,0:T(8,128)(2,1)S(1)}, u32[]{:S(2)}, u32[]{:S(2)}) collective-permute-start(bf16[176,256]{1,0:T(8,128)(2,1)S(1)} %get-tuple-element.35), channel_id=1, source_target_pairs={{0,4},{4,0},{8,12},{12,8},{1,5},{5,1},{9,13},{13,9},{2,6},{6,2},{1... | collective-permute-start | bytes 270344 | tf_op jit(solution)/shard_map/ppermute | solution.py:123
  15.3 7.1 %collective-permute-start.5 = (bf16[176,256]{1,0:T(8,128)(2,1)S(1)}, bf16[176,256]{1,0:T(8,128)(2,1)S(1)}, u32[]{:S(2)}, u32[]{:S(2)}) collective-permute-start(bf16[176,256]{1,0:T(8,128)(2,1)S(1)} %slice.4), channel_id=1, source_target_pairs={{0,4},{4,0},{8,12},{12,8},{1,5},{5,1},{9,13},{13,9},{2,6},{6,2},{1... | collective-permute-start | bytes 270344 | tf_op jit(solution)/shard_map/ppermute | solution.py:123
  25.7 5.0 %collective-permute-start.7 = (bf16[64,512]{1,0:T(8,128)(2,1)S(1)}, bf16[64,512]{1,0:T(8,128)(2,1)S(1)}, u32[]{:S(2)}, u32[]{:S(2)}) collective-permute-start(bf16[64,512]{1,0:T(8,128)(2,1)S(1)} %get-tuple-element.42), channel_id=1, source_target_pairs={{0,2},{2,0},{1,3},{3,1},{4,6},{6,4},{5,7},{7,5},{8,10},{10,8},{9,1... | collective-permute-start | bytes 196616 | tf_op jit(solution)/shard_map/ppermute | solution.py:118
  26.7 8.8 %collective-permute-start.20 = (bf16[80,512]{1,0:T(8,128)(2,1)S(1)}, bf16[80,512]{1,0:T(8,128)(2,1)S(1)}, u32[]{:S(2)}, u32[]{:S(2)}) collective-permute-start(bf16[80,512]{1,0:T(8,128)(2,1)S(1)} %get-tuple-element.41.names_ref), channel_id=1, source_target_pairs={{0,2},{2,0},{1,3},{3,1},{4,6},{6,4},{5,7},{7,5},{8,10},{10,8},{9,1... | collective-permute-start | bytes 245768 | tf_op jit(solution)/shard_map/ppermute | solution.py:118
  30.7 5.5 %collective-permute-start.8 = (bf16[64,512]{1,0:T(8,128)(2,1)S(1)}, bf16[64,512]{1,0:T(8,128)(2,1)S(1)}, u32[]{:S(2)}, u32[]{:S(2)}) collective-permute-start(bf16[64,512]{1,0:T(8,128)(2,1)S(1)} %get-tuple-element.44), channel_id=1, source_target_pairs={{0,4},{4,0},{8,12},{12,8},{1,5},{5,1},{9,13},{13,9},{2,6},{6,2},{1... | collective-permute-start | bytes 196616 | tf_op jit(solution)/shard_map/ppermute | solution.py:123
  31.0 9.4 %collective-permute-start.9 = (bf16[64,512]{1,0:T(8,128)(2,1)S(1)}, bf16[64,512]{1,0:T(8,128)(2,1)S(1)}, u32[]{:S(2)}, u32[]{:S(2)}) collective-permute-start(bf16[64,512]{1,0:T(8,128)(2,1)S(1)} %get-tuple-element.44), channel_id=1, source_target_pairs={{0,8},{4,12},{8,0},{12,4},{1,9},{5,13},{9,1},{13,5},{2,10},{6,14},... | collective-permute-start | bytes 196616 | tf_op jit(solution)/shard_map/ppermute | solution.py:123
  35.6 6.5 %collective-permute-start.10 = (bf16[64,512]{1,0:T(8,128)(2,1)S(1)}, bf16[64,512]{1,0:T(8,128)(2,1)S(1)}, u32[]{:S(2)}, u32[]{:S(2)}) collective-permute-start(bf16[64,512]{1,0:T(8,128)(2,1)S(1)} %get-tuple-element.44), channel_id=1, source_target_pairs={{0,12},{4,8},{8,4},{12,0},{1,13},{5,9},{9,5},{13,1},{2,14},{6,10},... | collective-permute-start | bytes 196616 | tf_op jit(solution)/shard_map/ppermute | solution.py:123
  35.6 6.4 %collective-permute-start.21 = (bf16[64,512]{1,0:T(8,128)(2,1)S(1)}, bf16[64,512]{1,0:T(8,128)(2,1)S(1)}, u32[]{:S(2)}, u32[]{:S(2)}) collective-permute-start(bf16[64,512]{1,0:T(8,128)(2,1)S(1)} %get-tuple-element.56), channel_id=1, source_target_pairs={{0,4},{4,0},{8,12},{12,8},{1,5},{5,1},{9,13},{13,9},{2,6},{6,2},{1... | collective-permute-start | bytes 196616 | tf_op jit(solution)/shard_map/ppermute | solution.py:123
  36.2 8.6 %collective-permute-start.22 = (bf16[64,512]{1,0:T(8,128)(2,1)S(1)}, bf16[64,512]{1,0:T(8,128)(2,1)S(1)}, u32[]{:S(2)}, u32[]{:S(2)}) collective-permute-start(bf16[64,512]{1,0:T(8,128)(2,1)S(1)} %get-tuple-element.56), channel_id=1, source_target_pairs={{0,8},{4,12},{8,0},{12,4},{1,9},{5,13},{9,1},{13,5},{2,10},{6,14},... | collective-permute-start | bytes 196616 | tf_op jit(solution)/shard_map/ppermute | solution.py:123
  40.4 6.1 %collective-permute-start.23 = (bf16[64,512]{1,0:T(8,128)(2,1)S(1)}, bf16[64,512]{1,0:T(8,128)(2,1)S(1)}, u32[]{:S(2)}, u32[]{:S(2)}) collective-permute-start(bf16[64,512]{1,0:T(8,128)(2,1)S(1)} %get-tuple-element.56), channel_id=1, source_target_pairs={{0,12},{4,8},{8,4},{12,0},{1,13},{5,9},{9,5},{13,1},{2,14},{6,10},... | collective-permute-start | bytes 196616 | tf_op jit(solution)/shard_map/ppermute | solution.py:123
  42.0 4.9 %collective-permute-start.25 = (bf16[64,512]{1,0:T(8,128)(2,1)S(1)}, bf16[64,512]{1,0:T(8,128)(2,1)S(1)}, u32[]{:S(2)}, u32[]{:S(2)}) collective-permute-start(bf16[64,512]{1,0:T(8,128)(2,1)S(1)} %collective-permute-done.21.refs_1_), channel_id=1, source_target_pairs={{0,1},{1,0},{2,3},{3,2},{4,5},{5,4},{6,7},{7,6},{8,9},{9,8},{10,11... | collective-permute-start | bytes 196616 | tf_op jit(solution)/shard_map/ppermute | solution.py:118
  51.3 4.7 %collective-permute-start.16 = (bf16[64,2048]{1,0:T(8,128)(2,1)S(1)}, bf16[64,2048]{1,0:T(8,128)(2,1)S(1)}, u32[]{:S(2)}, u32[]{:S(2)}) collective-permute-start(bf16[64,2048]{1,0:T(8,128)(2,1)S(1)} %get-tuple-element.49), channel_id=1, source_target_pairs={{0,1},{1,0},{2,3},{3,2},{4,5},{5,4},{6,7},{7,6},{8,9},{9,8},{10,11... | collective-permute-start | bytes 786440 | tf_op jit(solution)/shard_map/ppermute | solution.py:118
  51.6 6.0 %collective-permute-start.29 = (bf16[16,2048]{1,0:T(8,128)(2,1)S(1)}, bf16[16,2048]{1,0:T(8,128)(2,1)S(1)}, u32[]{:S(2)}, u32[]{:S(2)}) collective-permute-start(bf16[16,2048]{1,0:T(8,128)(2,1)S(1)} %get-tuple-element.60), channel_id=1, source_target_pairs={{0,4},{4,0},{8,12},{12,8},{1,5},{5,1},{9,13},{13,9},{2,6},{6,2},{1... | collective-permute-start | bytes 196616 | tf_op jit(solution)/shard_map/ppermute | solution.py:123
  51.6 10.4 %collective-permute-start.30 = (bf16[16,2048]{1,0:T(8,128)(2,1)S(1)}, bf16[16,2048]{1,0:T(8,128)(2,1)S(1)}, u32[]{:S(2)}, u32[]{:S(2)}) collective-permute-start(bf16[16,2048]{1,0:T(8,128)(2,1)S(1)} %get-tuple-element.61), channel_id=1, source_target_pairs={{0,8},{4,12},{8,0},{12,4},{1,9},{5,13},{9,1},{13,5},{2,10},{6,14},... | collective-permute-start | bytes 196616 | tf_op jit(solution)/shard_map/ppermute | solution.py:123
  53.6 8.4 %collective-permute-start.31 = (bf16[16,2048]{1,0:T(8,128)(2,1)S(1)}, bf16[16,2048]{1,0:T(8,128)(2,1)S(1)}, u32[]{:S(2)}, u32[]{:S(2)}) collective-permute-start(bf16[16,2048]{1,0:T(8,128)(2,1)S(1)} %get-tuple-element.62), channel_id=1, source_target_pairs={{0,12},{4,8},{8,4},{12,0},{1,13},{5,9},{9,5},{13,1},{2,14},{6,10},... | collective-permute-start | bytes 196616 | tf_op jit(solution)/shard_map/ppermute | solution.py:123
  56.1 8.3 %collective-permute-start.19 = (bf16[16,2048]{1,0:T(8,128)(2,1)S(1)}, bf16[16,2048]{1,0:T(8,128)(2,1)S(1)}, u32[]{:S(2)}, u32[]{:S(2)}) collective-permute-start(bf16[16,2048]{1,0:T(8,128)(2,1)S(1)} %get-tuple-element.53), channel_id=1, source_target_pairs={{0,12},{4,8},{8,4},{12,0},{1,13},{5,9},{9,5},{13,1},{2,14},{6,10},... | collective-permute-start | bytes 196616 | tf_op jit(solution)/shard_map/ppermute | solution.py:123
  57.6 9.2 %collective-permute-start.18 = (bf16[16,2048]{1,0:T(8,128)(2,1)S(1)}, bf16[16,2048]{1,0:T(8,128)(2,1)S(1)}, u32[]{:S(2)}, u32[]{:S(2)}) collective-permute-start(bf16[16,2048]{1,0:T(8,128)(2,1)S(1)} %get-tuple-element.52), channel_id=1, source_target_pairs={{0,8},{4,12},{8,0},{12,4},{1,9},{5,13},{9,1},{13,5},{2,10},{6,14},... | collective-permute-start | bytes 196616 | tf_op jit(solution)/shard_map/ppermute | solution.py:123
  57.6 9.2 %collective-permute-start.17 = (bf16[16,2048]{1,0:T(8,128)(2,1)S(1)}, bf16[16,2048]{1,0:T(8,128)(2,1)S(1)}, u32[]{:S(2)}, u32[]{:S(2)}) collective-permute-start(bf16[16,2048]{1,0:T(8,128)(2,1)S(1)} %get-tuple-element.51), channel_id=1, source_target_pairs={{0,4},{4,0},{8,12},{12,8},{1,5},{5,1},{9,13},{13,9},{2,6},{6,2},{1... | collective-permute-start | bytes 196616 | tf_op jit(solution)/shard_map/ppermute | solution.py:123
  62.1 4.7 %collective-permute-start.32 = (bf16[16,2048]{1,0:T(8,128)(2,1)S(1)}, bf16[16,2048]{1,0:T(8,128)(2,1)S(1)}, u32[]{:S(2)}, u32[]{:S(2)}) collective-permute-start(bf16[16,2048]{1,0:T(8,128)(2,1)S(1)} %shard_map.128), channel_id=1, source_target_pairs={{0,2},{2,0},{1,3},{3,1},{4,6},{6,4},{5,7},{7,5},{8,10},{10,8},{9,1... | collective-permute-start | bytes 196616 | tf_op jit(solution)/shard_map/ppermute | solution.py:118
  (20 other events, 199.2 us)

commit v3 on v2

--- a/solution.py
+++ b/solution.py
@@ -539,8 +539,10 @@
     row_count, top_count = expert_ids.shape
     capacity = max(2, row_count * top_count // router.shape[1] * 2)
     local_heads = queries.shape[1] // HEAD_DIM
-    one_each = operands[9].shape[0] == 1 and lax.axis_size("attn") == 4
-    if capacity >= row_count and one_each and local_heads <= HEADS // KV_HEADS:
+    one_each = operands[9].shape[0] == 1
+    sizes = tuple(lax.axis_size(n) for n in ("attn", "sect", "pair"))
+    exchanged = sizes == (4, 2, 2) and local_heads <= HEADS // KV_HEADS
+    if capacity >= row_count and one_each and exchanged:
         return dense_layer(*operands)
     return routed_layer(*operands)
 

time: 67.6 us -> 67.6 us (level)
  no operation moved by 1% of the time
where the time goes in v3:
time: 67.6 us; the launch traced here: 67.5 us
  starting transfers between devices  36.7 us (54%)
  waiting for transfers between devices  24.2 us (36%)
  Pallas kernels  4.85 us (7%)
  between operations  0.95 us (1%)
  other arithmetic  0.69 us (1%)
    ppermute x18, starting transfers between devices, swap(): return lax.ppermute(value, axis, [(i, i ^ mask) for i in range(size)])  28.3 us
    ppermute x18, waiting for transfers between devices, swap(): return lax.ppermute(value, axis, [(i, i ^ mask) for i in range(size)])  19.5 us
    ppermute x15, starting transfers between devices, rotate(): lax.ppermute(value, axis, [(i, (i + step) % size) for i in range(size)])  8.38 us
    pallas_call x11, Pallas kernels, call(): pl.pallas_call(kernel, out_shape=outs, in_specs=[VMEM] * len(operands), o...  4.85 us
    ppermute x15, waiting for transfers between devices, rotate(): lax.ppermute(value, axis, [(i, (i + step) % size) for i in range(size)])  4.71 us
  transfers between devices with their start and end apart: 33, of which 12 were waited for; matrix products, arithmetic and copies ran while one was open for 0% of the time, Pallas kernels for 7%

profile of v3, /device:TPU:0, one launch (start us, length us, event | category | flops | bytes accessed | tf_op | source)
XLA Modules:
  0.0 67.5 jit_solution(2254345972108318771)
XLA Ops:
  0.0 4.1 %collective-permute-start.1 = (bf16[64,1024]{1,0:T(8,128)(2,1)}, bf16[64,1024]{1,0:T(8,128)(2,1)S(1)}, u32[]{:S(2)}, u32[]{:S(2)}) collective-permute-start(bf16[64,1024]{1,0:T(8,128)(2,1)} %refs_0_.1), channel_id=1, source_target_pairs={{0,8},{4,12},{8,0},{12,4},{1,9},{5,13},{9,1},{13,5},{2,10},{6,14},... | collective-permute-start | bytes 393224 | tf_op jit(solution)/shard_map/ppermute | solution.py:123
  5.1 1.6 %collective-permute-start.15 = (bf16[384,1024]{1,0:T(8,128)(2,1)S(1)}, bf16[384,1024]{1,0:T(8,128)(2,1)S(1)}, u32[]{:S(2)}, u32[]{:S(2)}) collective-permute-start(bf16[384,1024]{1,0:T(8,128)(2,1)S(1)} %get-tuple-element.46), channel_id=1, source_target_pairs={{0,2},{2,0},{1,3},{3,1},{4,6},{6,4},{5,7},{7,5},{8,10},{10,8},{9,1... | collective-permute-start | bytes 2359304 | tf_op jit(solution)/shard_map/ppermute | solution.py:118
  7.3 1.6 %collective-permute-start = (bf16[64,1024]{1,0:T(8,128)(2,1)S(1)}, bf16[64,1024]{1,0:T(8,128)(2,1)S(1)}, u32[]{:S(2)}, u32[]{:S(2)}) collective-permute-start(bf16[64,1024]{1,0:T(8,128)(2,1)S(1)} %copy-done.3), channel_id=1, source_target_pairs={{0,4},{4,0},{8,12},{12,8},{1,5},{5,1},{9,13},{13,9},{2,6},{6,2},{1... | collective-permute-start | bytes 393224 | tf_op jit(solution)/shard_map/ppermute | solution.py:123
  8.9 4.3 %collective-permute-done.1.refs_2_ = bf16[64,1024]{1,0:T(8,128)(2,1)S(1)} collective-permute-done((bf16[64,1024]{1,0:T(8,128)(2,1)}, bf16[64,1024]{1,0:T(8,128)(2,1)S(1)}, u32[]{:S(2)}, u32[]{:S(2)}) %collective-permute-start.1) | collective-permute-done | bytes 131104 | tf_op jit(solution)/shard_map/ppermute | solution.py:123
  13.9 1.3 %collective-permute-start.3 = (bf16[176,256]{1,0:T(8,128)(2,1)S(1)}, bf16[176,256]{1,0:T(8,128)(2,1)S(1)}, u32[]{:S(2)}, u32[]{:S(2)}) collective-permute-start(bf16[176,256]{1,0:T(8,128)(2,1)S(1)} %get-tuple-element.35), channel_id=1, source_target_pairs={{0,4},{4,0},{8,12},{12,8},{1,5},{5,1},{9,13},{13,9},{2,6},{6,2},{1... | collective-permute-start | bytes 270344 | tf_op jit(solution)/shard_map/ppermute | solution.py:123
  16.1 5.4 %collective-permute-done.3.refs_5_ = bf16[176,256]{1,0:T(8,128)(2,1)S(1)} collective-permute-done((bf16[176,256]{1,0:T(8,128)(2,1)S(1)}, bf16[176,256]{1,0:T(8,128)(2,1)S(1)}, u32[]{:S(2)}, u32[]{:S(2)}) %collective-permute-start.3) | collective-permute-done | bytes 90144 | tf_op jit(solution)/shard_map/ppermute | solution.py:123
  22.4 1.6 %shard_map.120 = (f32[128,512]{1,0:T(8,128)S(1)}, f32[128,512]{1,0:T(8,128)S(1)}, bf16[16,512]{1,0:T(8,128)(2,1)S(1)}) custom-call(bf16[64,1024]{1,0:T(8,128)(2,1)S(1)} %copy-done.3, bf16[64,1024]{1,0:T(8,128)(2,1)S(1)} %collective-permute-done.refs_1_, bf16[64,1024]{1,0:T(8,128)(2,1)S(1)} %collective-permute-done.1.refs_2_, ...), custom_call_target="tpu_custom_call" | custom-call | flops 1048576 | bytes 1949696 | tf_op jit(solution)/shard_map/pallas_call | solution.py:390
  24.1 1.5 %collective-permute-done.6.refs_0_ = f32[128,512]{1,0:T(8,128)S(1)} collective-permute-done((f32[128,512]{1,0:T(8,128)S(1)}, f32[128,512]{1,0:T(8,128)S(1)}, u32[]{:S(2)}, u32[]{:S(2)}) %collective-permute-start.6) | collective-permute-done | bytes 262176 | tf_op jit(solution)/shard_map/ppermute | solution.py:118
  25.7 1.1 %collective-permute-start.7 = (bf16[64,512]{1,0:T(8,128)(2,1)S(1)}, bf16[64,512]{1,0:T(8,128)(2,1)S(1)}, u32[]{:S(2)}, u32[]{:S(2)}) collective-permute-start(bf16[64,512]{1,0:T(8,128)(2,1)S(1)} %get-tuple-element.42), channel_id=1, source_target_pairs={{0,2},{2,0},{1,3},{3,1},{4,6},{6,4},{5,7},{7,5},{8,10},{10,8},{9,1... | collective-permute-start | bytes 196616 | tf_op jit(solution)/shard_map/ppermute | solution.py:118
  26.7 1.0 %collective-permute-start.20 = (bf16[80,512]{1,0:T(8,128)(2,1)S(1)}, bf16[80,512]{1,0:T(8,128)(2,1)S(1)}, u32[]{:S(2)}, u32[]{:S(2)}) collective-permute-start(bf16[80,512]{1,0:T(8,128)(2,1)S(1)} %get-tuple-element.41.names_ref), channel_id=1, source_target_pairs={{0,2},{2,0},{1,3},{3,1},{4,6},{6,4},{5,7},{7,5},{8,10},{10,8},{9,1... | collective-permute-start | bytes 245768 | tf_op jit(solution)/shard_map/ppermute | solution.py:118
  27.8 2.9 %collective-permute-done.7.refs_0_ = bf16[64,512]{1,0:T(8,128)(2,1)S(1)} collective-permute-done((bf16[64,512]{1,0:T(8,128)(2,1)S(1)}, bf16[64,512]{1,0:T(8,128)(2,1)S(1)}, u32[]{:S(2)}, u32[]{:S(2)}) %collective-permute-start.7) | collective-permute-done | bytes 65568 | tf_op jit(solution)/shard_map/ppermute | solution.py:118
  31.0 4.6 %collective-permute-start.9 = (bf16[64,512]{1,0:T(8,128)(2,1)S(1)}, bf16[64,512]{1,0:T(8,128)(2,1)S(1)}, u32[]{:S(2)}, u32[]{:S(2)}) collective-permute-start(bf16[64,512]{1,0:T(8,128)(2,1)S(1)} %get-tuple-element.44), channel_id=1, source_target_pairs={{0,8},{4,12},{8,0},{12,4},{1,9},{5,13},{9,1},{13,5},{2,10},{6,14},... | collective-permute-start | bytes 196616 | tf_op jit(solution)/shard_map/ppermute | solution.py:123
  36.2 3.8 %collective-permute-start.22 = (bf16[64,512]{1,0:T(8,128)(2,1)S(1)}, bf16[64,512]{1,0:T(8,128)(2,1)S(1)}, u32[]{:S(2)}, u32[]{:S(2)}) collective-permute-start(bf16[64,512]{1,0:T(8,128)(2,1)S(1)} %get-tuple-element.56), channel_id=1, source_target_pairs={{0,8},{4,12},{8,0},{12,4},{1,9},{5,13},{9,1},{13,5},{2,10},{6,14},... | collective-permute-start | bytes 196616 | tf_op jit(solution)/shard_map/ppermute | solution.py:123
  42.6 2.3 %collective-permute-done.22.refs_2_ = bf16[64,512]{1,0:T(8,128)(2,1)S(1)} collective-permute-done((bf16[64,512]{1,0:T(8,128)(2,1)S(1)}, bf16[64,512]{1,0:T(8,128)(2,1)S(1)}, u32[]{:S(2)}, u32[]{:S(2)}) %collective-permute-start.22) | collective-permute-done | bytes 65568 | tf_op jit(solution)/shard_map/ppermute | solution.py:123
  44.8 1.6 %collective-permute-done.23.refs_3_ = bf16[64,512]{1,0:T(8,128)(2,1)S(1)} collective-permute-done((bf16[64,512]{1,0:T(8,128)(2,1)S(1)}, bf16[64,512]{1,0:T(8,128)(2,1)S(1)}, u32[]{:S(2)}, u32[]{:S(2)}) %collective-permute-start.23) | collective-permute-done | bytes 65568 | tf_op jit(solution)/shard_map/ppermute | solution.py:123
  47.9 1.5 %shard_map.126 = (f32[64,2048]{1,0:T(8,128)S(1)}, bf16[64,2048]{1,0:T(8,128)(2,1)S(1)}) custom-call(bf16[80,512]{1,0:T(8,128)(2,1)S(1)} %get-tuple-element.55.refs_0_, bf16[64,512]{1,0:T(8,128)(2,1)S(1)} %collective-permute-done.21.refs_1_, bf16[64,512]{1,0:T(8,128)(2,1)S(1)} %collective-permute-done.22.refs_2_, ...), custom_call_target="tpu_custom_call" | custom-call | flops 2147483648 | bytes 5316608 | tf_op jit(solution)/shard_map/pallas_call | solution.py:390
  49.8 1.5 %shard_map.123 = (f32[64,2048]{1,0:T(8,128)S(1)}, bf16[64,2048]{1,0:T(8,128)(2,1)S(1)}, bf16[16,2048]{1,0:T(8,128)(2,1)S(1)}) custom-call(bf16[80,512]{1,0:T(8,128)(2,1)S(1)} %get-tuple-element.43.refs_0_, bf16[64,512]{1,0:T(8,128)(2,1)S(1)} %collective-permute-done.8.refs_1_, bf16[64,512]{1,0:T(8,128)(2,1)S(1)} %collective-permute-done.9.refs_2_, ...), custom_call_target="tpu_custom_call" | custom-call | flops 2147483648 | bytes 5316608 | tf_op jit(solution)/shard_map/pallas_call | solution.py:390
  51.6 2.0 %collective-permute-start.30 = (bf16[16,2048]{1,0:T(8,128)(2,1)S(1)}, bf16[16,2048]{1,0:T(8,128)(2,1)S(1)}, u32[]{:S(2)}, u32[]{:S(2)}) collective-permute-start(bf16[16,2048]{1,0:T(8,128)(2,1)S(1)} %get-tuple-element.61), channel_id=1, source_target_pairs={{0,8},{4,12},{8,0},{12,4},{1,9},{5,13},{9,1},{13,5},{2,10},{6,14},... | collective-permute-start | bytes 196616 | tf_op jit(solution)/shard_map/ppermute | solution.py:123
  53.6 2.4 %collective-permute-start.31 = (bf16[16,2048]{1,0:T(8,128)(2,1)S(1)}, bf16[16,2048]{1,0:T(8,128)(2,1)S(1)}, u32[]{:S(2)}, u32[]{:S(2)}) collective-permute-start(bf16[16,2048]{1,0:T(8,128)(2,1)S(1)} %get-tuple-element.62), channel_id=1, source_target_pairs={{0,12},{4,8},{8,4},{12,0},{1,13},{5,9},{9,5},{13,1},{2,14},{6,10},... | collective-permute-start | bytes 196616 | tf_op jit(solution)/shard_map/ppermute | solution.py:123
  56.1 1.5 %collective-permute-start.19 = (bf16[16,2048]{1,0:T(8,128)(2,1)S(1)}, bf16[16,2048]{1,0:T(8,128)(2,1)S(1)}, u32[]{:S(2)}, u32[]{:S(2)}) collective-permute-start(bf16[16,2048]{1,0:T(8,128)(2,1)S(1)} %get-tuple-element.53), channel_id=1, source_target_pairs={{0,12},{4,8},{8,4},{12,0},{1,13},{5,9},{9,5},{13,1},{2,14},{6,10},... | collective-permute-start | bytes 196616 | tf_op jit(solution)/shard_map/ppermute | solution.py:123
  57.6 2.9 %collective-permute-start.17 = (bf16[16,2048]{1,0:T(8,128)(2,1)S(1)}, bf16[16,2048]{1,0:T(8,128)(2,1)S(1)}, u32[]{:S(2)}, u32[]{:S(2)}) collective-permute-start(bf16[16,2048]{1,0:T(8,128)(2,1)S(1)} %get-tuple-element.51), channel_id=1, source_target_pairs={{0,4},{4,0},{8,12},{12,8},{1,5},{5,1},{9,13},{13,9},{2,6},{6,2},{1... | collective-permute-start | bytes 196616 | tf_op jit(solution)/shard_map/ppermute | solution.py:123
  60.5 1.5 %collective-permute-done.30.refs_1_ = bf16[16,2048]{1,0:T(8,128)(2,1)S(1)} collective-permute-done((bf16[16,2048]{1,0:T(8,128)(2,1)S(1)}, bf16[16,2048]{1,0:T(8,128)(2,1)S(1)}, u32[]{:S(2)}, u32[]{:S(2)}) %collective-permute-start.30) | collective-permute-done | bytes 65568 | tf_op jit(solution)/shard_map/ppermute | solution.py:123
  62.1 2.3 %collective-permute-start.32 = (bf16[16,2048]{1,0:T(8,128)(2,1)S(1)}, bf16[16,2048]{1,0:T(8,128)(2,1)S(1)}, u32[]{:S(2)}, u32[]{:S(2)}) collective-permute-start(bf16[16,2048]{1,0:T(8,128)(2,1)S(1)} %shard_map.128), channel_id=1, source_target_pairs={{0,2},{2,0},{1,3},{3,1},{4,6},{6,4},{5,7},{7,5},{8,10},{10,8},{9,1... | collective-permute-start | bytes 196616 | tf_op jit(solution)/shard_map/ppermute | solution.py:118
  64.4 2.4 %collective-permute-done.18 = bf16[16,2048]{1,0:T(8,128)(2,1)S(1)} collective-permute-done((bf16[16,2048]{1,0:T(8,128)(2,1)S(1)}, bf16[16,2048]{1,0:T(8,128)(2,1)S(1)}, u32[]{:S(2)}, u32[]{:S(2)}) %collective-permute-start.18) | collective-permute-done | bytes 65568 | tf_op jit(solution)/shard_map/ppermute | solution.py:123
  (77 shorter events, 9.8 us)
Async XLA Ops:
  0.0 13.2 %collective-permute-start.1 = (bf16[64,1024]{1,0:T(8,128)(2,1)}, bf16[64,1024]{1,0:T(8,128)(2,1)S(1)}, u32[]{:S(2)}, u32[]{:S(2)}) collective-permute-start(bf16[64,1024]{1,0:T(8,128)(2,1)} %refs_0_.1), channel_id=1, source_target_pairs={{0,8},{4,12},{8,0},{12,4},{1,9},{5,13},{9,1},{13,5},{2,10},{6,14},... | collective-permute-start | bytes 393224 | tf_op jit(solution)/shard_map/ppermute | solution.py:123
  5.1 42.8 %collective-permute-start.15 = (bf16[384,1024]{1,0:T(8,128)(2,1)S(1)}, bf16[384,1024]{1,0:T(8,128)(2,1)S(1)}, u32[]{:S(2)}, u32[]{:S(2)}) collective-permute-start(bf16[384,1024]{1,0:T(8,128)(2,1)S(1)} %get-tuple-element.46), channel_id=1, source_target_pairs={{0,2},{2,0},{1,3},{3,1},{4,6},{6,4},{5,7},{7,5},{8,10},{10,8},{9,1... | collective-permute-start | bytes 2359304 | tf_op jit(solution)/shard_map/ppermute | solution.py:118
  6.7 8.6 %collective-permute-start.4 = (bf16[208,256]{1,0:T(8,128)(2,1)S(1)}, bf16[208,256]{1,0:T(8,128)(2,1)S(1)}, u32[]{:S(2)}, u32[]{:S(2)}) collective-permute-start(bf16[208,256]{1,0:T(8,128)(2,1)S(1)} %get-tuple-element.36), channel_id=1, source_target_pairs={{0,8},{4,12},{8,0},{12,4},{1,9},{5,13},{9,1},{13,5},{2,10},{6,14},... | collective-permute-start | bytes 319496 | tf_op jit(solution)/shard_map/ppermute | solution.py:123
  7.3 14.2 %collective-permute-start = (bf16[64,1024]{1,0:T(8,128)(2,1)S(1)}, bf16[64,1024]{1,0:T(8,128)(2,1)S(1)}, u32[]{:S(2)}, u32[]{:S(2)}) collective-permute-start(bf16[64,1024]{1,0:T(8,128)(2,1)S(1)} %copy-done.3), channel_id=1, source_target_pairs={{0,4},{4,0},{8,12},{12,8},{1,5},{5,1},{9,13},{13,9},{2,6},{6,2},{1... | collective-permute-start | bytes 393224 | tf_op jit(solution)/shard_map/ppermute | solution.py:123
  13.2 9.3 %collective-permute-start.2 = (bf16[64,1024]{1,0:T(8,128)(2,1)S(1)}, bf16[64,1024]{1,0:T(8,128)(2,1)S(1)}, u32[]{:S(2)}, u32[]{:S(2)}) collective-permute-start(bf16[64,1024]{1,0:T(8,128)(2,1)S(1)} %collective-permute-done.1.refs_2_), channel_id=1, source_target_pairs={{0,4},{4,0},{8,12},{12,8},{1,5},{5,1},{9,13},{13,9},{2,6},{6,2},{1... | collective-permute-start | bytes 393224 | tf_op jit(solution)/shard_map/ppermute | solution.py:123
  13.9 7.6 %collective-permute-start.3 = (bf16[176,256]{1,0:T(8,128)(2,1)S(1)}, bf16[176,256]{1,0:T(8,128)(2,1)S(1)}, u32[]{:S(2)}, u32[]{:S(2)}) collective-permute-start(bf16[176,256]{1,0:T(8,128)(2,1)S(1)} %get-tuple-element.35), channel_id=1, source_target_pairs={{0,4},{4,0},{8,12},{12,8},{1,5},{5,1},{9,13},{13,9},{2,6},{6,2},{1... | collective-permute-start | bytes 270344 | tf_op jit(solution)/shard_map/ppermute | solution.py:123
  15.3 7.1 %collective-permute-start.5 = (bf16[176,256]{1,0:T(8,128)(2,1)S(1)}, bf16[176,256]{1,0:T(8,128)(2,1)S(1)}, u32[]{:S(2)}, u32[]{:S(2)}) collective-permute-start(bf16[176,256]{1,0:T(8,128)(2,1)S(1)} %slice.4), channel_id=1, source_target_pairs={{0,4},{4,0},{8,12},{12,8},{1,5},{5,1},{9,13},{13,9},{2,6},{6,2},{1... | collective-permute-start | bytes 270344 | tf_op jit(solution)/shard_map/ppermute | solution.py:123
  25.7 5.0 %collective-permute-start.7 = (bf16[64,512]{1,0:T(8,128)(2,1)S(1)}, bf16[64,512]{1,0:T(8,128)(2,1)S(1)}, u32[]{:S(2)}, u32[]{:S(2)}) collective-permute-start(bf16[64,512]{1,0:T(8,128)(2,1)S(1)} %get-tuple-element.42), channel_id=1, source_target_pairs={{0,2},{2,0},{1,3},{3,1},{4,6},{6,4},{5,7},{7,5},{8,10},{10,8},{9,1... | collective-permute-start | bytes 196616 | tf_op jit(solution)/shard_map/ppermute | solution.py:118
  26.7 8.8 %collective-permute-start.20 = (bf16[80,512]{1,0:T(8,128)(2,1)S(1)}, bf16[80,512]{1,0:T(8,128)(2,1)S(1)}, u32[]{:S(2)}, u32[]{:S(2)}) collective-permute-start(bf16[80,512]{1,0:T(8,128)(2,1)S(1)} %get-tuple-element.41.names_ref), channel_id=1, source_target_pairs={{0,2},{2,0},{1,3},{3,1},{4,6},{6,4},{5,7},{7,5},{8,10},{10,8},{9,1... | collective-permute-start | bytes 245768 | tf_op jit(solution)/shard_map/ppermute | solution.py:118
  30.7 5.5 %collective-permute-start.8 = (bf16[64,512]{1,0:T(8,128)(2,1)S(1)}, bf16[64,512]{1,0:T(8,128)(2,1)S(1)}, u32[]{:S(2)}, u32[]{:S(2)}) collective-permute-start(bf16[64,512]{1,0:T(8,128)(2,1)S(1)} %get-tuple-element.44), channel_id=1, source_target_pairs={{0,4},{4,0},{8,12},{12,8},{1,5},{5,1},{9,13},{13,9},{2,6},{6,2},{1... | collective-permute-start | bytes 196616 | tf_op jit(solution)/shard_map/ppermute | solution.py:123
  31.0 9.4 %collective-permute-start.9 = (bf16[64,512]{1,0:T(8,128)(2,1)S(1)}, bf16[64,512]{1,0:T(8,128)(2,1)S(1)}, u32[]{:S(2)}, u32[]{:S(2)}) collective-permute-start(bf16[64,512]{1,0:T(8,128)(2,1)S(1)} %get-tuple-element.44), channel_id=1, source_target_pairs={{0,8},{4,12},{8,0},{12,4},{1,9},{5,13},{9,1},{13,5},{2,10},{6,14},... | collective-permute-start | bytes 196616 | tf_op jit(solution)/shard_map/ppermute | solution.py:123
  35.6 6.5 %collective-permute-start.10 = (bf16[64,512]{1,0:T(8,128)(2,1)S(1)}, bf16[64,512]{1,0:T(8,128)(2,1)S(1)}, u32[]{:S(2)}, u32[]{:S(2)}) collective-permute-start(bf16[64,512]{1,0:T(8,128)(2,1)S(1)} %get-tuple-element.44), channel_id=1, source_target_pairs={{0,12},{4,8},{8,4},{12,0},{1,13},{5,9},{9,5},{13,1},{2,14},{6,10},... | collective-permute-start | bytes 196616 | tf_op jit(solution)/shard_map/ppermute | solution.py:123
  35.6 6.4 %collective-permute-start.21 = (bf16[64,512]{1,0:T(8,128)(2,1)S(1)}, bf16[64,512]{1,0:T(8,128)(2,1)S(1)}, u32[]{:S(2)}, u32[]{:S(2)}) collective-permute-start(bf16[64,512]{1,0:T(8,128)(2,1)S(1)} %get-tuple-element.56), channel_id=1, source_target_pairs={{0,4},{4,0},{8,12},{12,8},{1,5},{5,1},{9,13},{13,9},{2,6},{6,2},{1... | collective-permute-start | bytes 196616 | tf_op jit(solution)/shard_map/ppermute | solution.py:123
  36.2 8.6 %collective-permute-start.22 = (bf16[64,512]{1,0:T(8,128)(2,1)S(1)}, bf16[64,512]{1,0:T(8,128)(2,1)S(1)}, u32[]{:S(2)}, u32[]{:S(2)}) collective-permute-start(bf16[64,512]{1,0:T(8,128)(2,1)S(1)} %get-tuple-element.56), channel_id=1, source_target_pairs={{0,8},{4,12},{8,0},{12,4},{1,9},{5,13},{9,1},{13,5},{2,10},{6,14},... | collective-permute-start | bytes 196616 | tf_op jit(solution)/shard_map/ppermute | solution.py:123
  40.4 6.1 %collective-permute-start.23 = (bf16[64,512]{1,0:T(8,128)(2,1)S(1)}, bf16[64,512]{1,0:T(8,128)(2,1)S(1)}, u32[]{:S(2)}, u32[]{:S(2)}) collective-permute-start(bf16[64,512]{1,0:T(8,128)(2,1)S(1)} %get-tuple-element.56), channel_id=1, source_target_pairs={{0,12},{4,8},{8,4},{12,0},{1,13},{5,9},{9,5},{13,1},{2,14},{6,10},... | collective-permute-start | bytes 196616 | tf_op jit(solution)/shard_map/ppermute | solution.py:123
  42.0 4.9 %collective-permute-start.25 = (bf16[64,512]{1,0:T(8,128)(2,1)S(1)}, bf16[64,512]{1,0:T(8,128)(2,1)S(1)}, u32[]{:S(2)}, u32[]{:S(2)}) collective-permute-start(bf16[64,512]{1,0:T(8,128)(2,1)S(1)} %collective-permute-done.21.refs_1_), channel_id=1, source_target_pairs={{0,1},{1,0},{2,3},{3,2},{4,5},{5,4},{6,7},{7,6},{8,9},{9,8},{10,11... | collective-permute-start | bytes 196616 | tf_op jit(solution)/shard_map/ppermute | solution.py:118
  51.3 4.7 %collective-permute-start.16 = (bf16[64,2048]{1,0:T(8,128)(2,1)S(1)}, bf16[64,2048]{1,0:T(8,128)(2,1)S(1)}, u32[]{:S(2)}, u32[]{:S(2)}) collective-permute-start(bf16[64,2048]{1,0:T(8,128)(2,1)S(1)} %get-tuple-element.49), channel_id=1, source_target_pairs={{0,1},{1,0},{2,3},{3,2},{4,5},{5,4},{6,7},{7,6},{8,9},{9,8},{10,11... | collective-permute-start | bytes 786440 | tf_op jit(solution)/shard_map/ppermute | solution.py:118
  51.6 6.0 %collective-permute-start.29 = (bf16[16,2048]{1,0:T(8,128)(2,1)S(1)}, bf16[16,2048]{1,0:T(8,128)(2,1)S(1)}, u32[]{:S(2)}, u32[]{:S(2)}) collective-permute-start(bf16[16,2048]{1,0:T(8,128)(2,1)S(1)} %get-tuple-element.60), channel_id=1, source_target_pairs={{0,4},{4,0},{8,12},{12,8},{1,5},{5,1},{9,13},{13,9},{2,6},{6,2},{1... | collective-permute-start | bytes 196616 | tf_op jit(solution)/shard_map/ppermute | solution.py:123
  51.6 10.4 %collective-permute-start.30 = (bf16[16,2048]{1,0:T(8,128)(2,1)S(1)}, bf16[16,2048]{1,0:T(8,128)(2,1)S(1)}, u32[]{:S(2)}, u32[]{:S(2)}) collective-permute-start(bf16[16,2048]{1,0:T(8,128)(2,1)S(1)} %get-tuple-element.61), channel_id=1, source_target_pairs={{0,8},{4,12},{8,0},{12,4},{1,9},{5,13},{9,1},{13,5},{2,10},{6,14},... | collective-permute-start | bytes 196616 | tf_op jit(solution)/shard_map/ppermute | solution.py:123
  53.6 8.4 %collective-permute-start.31 = (bf16[16,2048]{1,0:T(8,128)(2,1)S(1)}, bf16[16,2048]{1,0:T(8,128)(2,1)S(1)}, u32[]{:S(2)}, u32[]{:S(2)}) collective-permute-start(bf16[16,2048]{1,0:T(8,128)(2,1)S(1)} %get-tuple-element.62), channel_id=1, source_target_pairs={{0,12},{4,8},{8,4},{12,0},{1,13},{5,9},{9,5},{13,1},{2,14},{6,10},... | collective-permute-start | bytes 196616 | tf_op jit(solution)/shard_map/ppermute | solution.py:123
  56.1 8.3 %collective-permute-start.19 = (bf16[16,2048]{1,0:T(8,128)(2,1)S(1)}, bf16[16,2048]{1,0:T(8,128)(2,1)S(1)}, u32[]{:S(2)}, u32[]{:S(2)}) collective-permute-start(bf16[16,2048]{1,0:T(8,128)(2,1)S(1)} %get-tuple-element.53), channel_id=1, source_target_pairs={{0,12},{4,8},{8,4},{12,0},{1,13},{5,9},{9,5},{13,1},{2,14},{6,10},... | collective-permute-start | bytes 196616 | tf_op jit(solution)/shard_map/ppermute | solution.py:123
  57.6 9.2 %collective-permute-start.18 = (bf16[16,2048]{1,0:T(8,128)(2,1)S(1)}, bf16[16,2048]{1,0:T(8,128)(2,1)S(1)}, u32[]{:S(2)}, u32[]{:S(2)}) collective-permute-start(bf16[16,2048]{1,0:T(8,128)(2,1)S(1)} %get-tuple-element.52), channel_id=1, source_target_pairs={{0,8},{4,12},{8,0},{12,4},{1,9},{5,13},{9,1},{13,5},{2,10},{6,14},... | collective-permute-start | bytes 196616 | tf_op jit(solution)/shard_map/ppermute | solution.py:123
  57.6 9.2 %collective-permute-start.17 = (bf16[16,2048]{1,0:T(8,128)(2,1)S(1)}, bf16[16,2048]{1,0:T(8,128)(2,1)S(1)}, u32[]{:S(2)}, u32[]{:S(2)}) collective-permute-start(bf16[16,2048]{1,0:T(8,128)(2,1)S(1)} %get-tuple-element.51), channel_id=1, source_target_pairs={{0,4},{4,0},{8,12},{12,8},{1,5},{5,1},{9,13},{13,9},{2,6},{6,2},{1... | collective-permute-start | bytes 196616 | tf_op jit(solution)/shard_map/ppermute | solution.py:123
  62.1 4.7 %collective-permute-start.32 = (bf16[16,2048]{1,0:T(8,128)(2,1)S(1)}, bf16[16,2048]{1,0:T(8,128)(2,1)S(1)}, u32[]{:S(2)}, u32[]{:S(2)}) collective-permute-start(bf16[16,2048]{1,0:T(8,128)(2,1)S(1)} %shard_map.128), channel_id=1, source_target_pairs={{0,2},{2,0},{1,3},{3,1},{4,6},{6,4},{5,7},{7,5},{8,10},{10,8},{9,1... | collective-permute-start | bytes 196616 | tf_op jit(solution)/shard_map/ppermute | solution.py:118
  (20 other events, 199.2 us)
